TPU v7x, 32 devices: a whole 2x2x4 slice. The times are simulated.
32 devices in a mesh: rows: 8 (over z, x), cores: 4 (over y, core).
Axes of the slice: x: 2, y: 2, z: 4, core: 2. Of those that a mesh axis runs over, the one named last changes fastest.
Arguments:
- factor_one: bfloat16 [65536, 256], P(('rows', 'cores')), may hold values from -0.375 to 0.375
- factor_two: bfloat16 [65536, 256], P(('rows', 'cores')), may hold values from -0.375 to 0.375
- middle_one: float32 [256, 256], replicated, may hold values from -0.375 to 0.375
- middle_two: float32 [256, 256], replicated, may hold values from -0.375 to 0.375
- directions: float32 [8, 65536], P(None, ('rows', 'cores')), may hold values from -6 to 6
- residual: float32 [8, 65536], P(None, ('rows', 'cores')), may hold values from -6 to 6
Outputs:
- products: float32 [8, 65536], P(None, ('rows', 'cores'))
- gradient: float32 [65536, 256], P(('rows', 'cores'))
All inputs are finite; a program needn't handle non-finite values.
Results may differ from a plain program's by a relative error of at most 0.0041.
Values sent between devices are 32-bit elements; how exact they have to be, the bound alone decides.
No kernel may reach another device: no remote copies, remote signals or barrier semaphores. Data moves between devices by JAX's collectives and lax.ppermute only.
A program may use at most 64 MiB of HBM per device.

v0:
```python
import functools
import jax
import jax.numpy as jnp
from jax import lax
from jax.experimental import pallas as pl
from jax.experimental.pallas import tpu as pltpu
from jax.sharding import PartitionSpec as P


AXES = ("rows", "cores")
VMEM = pl.BlockSpec(memory_space=pltpu.VMEM)
SMEM = pl.BlockSpec(memory_space=pltpu.SMEM)
TILE = 256
LOADS = 4
STAGES = ((0,), (1, 2), (3,))

GROUPS = ((3, (2, 1, 3, 4), "h"), (3, (1, 3, 2, 4), "h"), (2, (3, 2, 4, 1), "d"))

NT = (((1,), (1,)), ((), ()))


def bit_of(me, bit):
    return lax.rem(lax.shift_right_logical(me, bit), 2)


def split(x):
    high = x.astype(jnp.bfloat16)
    return high, (x - high.astype(jnp.float32)).astype(jnp.bfloat16)


def dot3(a, b):
    dot = functools.partial(lax.dot_general, dimension_numbers=NT, preferred_element_type=jnp.float32)
    return dot(a[0], b[0]) + (dot(a[0], b[1]) + dot(a[1], b[0]))


def blocks(count, mode, rank):
    quarter = rank // 4
    if mode == "d":
        return [(m * quarter, quarter, (), m) for m in range(count)]
    half = quarter // 2
    return [((r3 * count + m) * half, half, (r3,), m) for r3 in range(2) for m in range(count)]


def offset(me, bits, rel, block):
    total = 0
    size = block
    for bit, r in zip(bits, rel):
        size //= 2
        mine = bit_of(me, bit)
        total = total + (mine if r == 0 else 1 - mine) * size
    return total


def weighted(items, base, dirs_ref, res_ref, f2t, rows):
    parts = []
    for kind, probe in items:
        w = (dirs_ref if kind == 0 else res_ref)[pl.ds(base + probe, 1), rows]
        parts.append((f2t * w).astype(jnp.bfloat16))
    return jnp.concatenate(parts, axis=0)


def open_kernel(items, half, s_ref, f1_in, f2_in, dirs_in, res_in, out_ref, f1_ref, f2t_ref, dirs_ref, res_ref, f2_ref, sems):
    base = (1 - bit_of(s_ref[0], 0)) * half
    size = f1_in.shape[0] // LOADS
    small = [
        pltpu.make_async_copy(dirs_in, dirs_ref, sems.at[0]),
        pltpu.make_async_copy(res_in, res_ref, sems.at[1]),
    ]
    big = []
    for i in range(LOADS):
        part = pl.ds(i * size, size)
        big.append((
            pltpu.make_async_copy(f2_in.at[part], f2_ref.at[part], sems.at[2 + 2 * i]),
            pltpu.make_async_copy(f1_in.at[part], f1_ref.at[part], sems.at[3 + 2 * i]),
        ))
    for copy in small + [c for two in big for c in two]:
        copy.start()
    for copy in small:
        copy.wait()
    for k in range(f1_in.shape[0] // TILE):
        if k * TILE % size == 0:
            for copy in big[k * TILE // size]:
                copy.wait()
        rows = pl.ds(k * TILE, TILE)
        f2t = f2_ref[rows, :].astype(jnp.float32).T
        f2t_ref[:, rows] = f2t.astype(jnp.bfloat16)
        st = weighted(items, base, dirs_ref, res_ref, f2t, rows)
        r = jnp.dot(st, f1_ref[rows, :], preferred_element_type=jnp.float32)
        if k == 0:
            out_ref[...] = r
        else:
            out_ref[...] += r


def open_build(items, half, me, f1, f2, dirs, res):
    n, rank = f1.shape
    m = len(items)
    hbm = pl.BlockSpec(memory_space=pltpu.HBM)
    return pl.pallas_call(
        functools.partial(open_kernel, items, half),
        out_shape=[
            jax.ShapeDtypeStruct((m * rank, rank), jnp.float32),
            jax.ShapeDtypeStruct((n, rank), jnp.bfloat16),
            jax.ShapeDtypeStruct((rank, n), jnp.bfloat16),
            jax.ShapeDtypeStruct(dirs.shape, jnp.float32),
            jax.ShapeDtypeStruct(res.shape, jnp.float32),
        ],
        in_specs=[SMEM] + [hbm] * 4,
        out_specs=[VMEM] * 5,
        scratch_shapes=[pltpu.VMEM((n, rank), jnp.bfloat16), pltpu.SemaphoreType.DMA((2 + 2 * LOADS,))],
        compiler_params=pltpu.CompilerParams(vmem_limit_bytes=10 << 20),
        name="cores_open",
        cost_estimate=pl.CostEstimate(flops=2 * m * n * rank * rank, bytes_accessed=n * rank * 4, transcendentals=0),
    )(me, *(pltpu.with_memory_space_constraint(x, pltpu.HBM) for x in (f1, f2, dirs, res)))


def core_kernel(items, mine, half, s_ref, f1_ref, f2t_ref, dirs_ref, res_ref, *refs):
    out_ref = refs[-1]
    core = bit_of(s_ref[0], 0)
    base = (core if mine else 1 - core) * half
    for k in range(f1_ref.shape[0] // TILE):
        rows = pl.ds(k * TILE, TILE)
        st = weighted(items, base, dirs_ref, res_ref, f2t_ref[:, rows].astype(jnp.float32), rows)
        r = jnp.dot(st, f1_ref[rows, :], preferred_element_type=jnp.float32)
        if k == 0:
            out_ref[...] = r
        else:
            out_ref[...] += r


def build(items, mine, half, after, me, f1, f2t, dirs, res):
    n, rank = f1.shape
    m = len(items)
    extra = [] if after is None else [after]
    return pl.pallas_call(
        functools.partial(core_kernel, items, mine, half),
        out_shape=jax.ShapeDtypeStruct((m * rank, rank), jnp.float32),
        in_specs=[SMEM] + [VMEM] * 4 + [pl.BlockSpec(memory_space=pl.ANY)] * len(extra),
        out_specs=VMEM,
        compiler_params=pltpu.CompilerParams(vmem_limit_bytes=8 << 20),
        cost_estimate=pl.CostEstimate(flops=2 * m * n * rank * rank, bytes_accessed=n * rank * 4, transcendentals=0),
    )(me, f1, f2t, dirs, res, *extra)


def left_kernel(items, bits, mode, s_ref, a_ref, b_ref, m1_ref, q0, q1, q2, q3, scr):
    me = s_ref[0]
    qs = (q0, q1, q2, q3)
    rank = m1_ref.shape[0]
    m = len(items)
    m1 = m1_ref[...]
    sides = (split(m1), split(m1.T))
    for j, (kind, _) in enumerate(items):
        ct = a_ref[j * rank:(j + 1) * rank, :] + b_ref[j * rank:(j + 1) * rank, :]
        scr[j * rank:(j + 1) * rank, :] = dot3(sides[kind], split(ct))
    for r1 in range(2):
        for r2 in range(2):
            for row, size, r3, j in blocks(m, mode, rank):
                off = pl.multiple_of(offset(me, bits, (r1, r2) + r3, rank), 32)
                qs[r1 * 2 + r2][row:row + size, :] = scr[pl.ds(j * rank + off, size), :]


def left(items, bits, mode, me, own, got, m1):
    rank = m1.shape[0]
    m = len(items)
    return pl.pallas_call(
        functools.partial(left_kernel, items, bits, mode),
        out_shape=[jax.ShapeDtypeStruct((m * rank // 4, rank), jnp.float32)] * 4,
        in_specs=[SMEM] + [VMEM] * 3,
        out_specs=[VMEM] * 4,
        scratch_shapes=[pltpu.VMEM((m * rank, rank), jnp.float32)],
        compiler_params=pltpu.CompilerParams(vmem_limit_bytes=8 << 20),
        name="left",
        cost_estimate=pl.CostEstimate(flops=6 * m * rank**3, bytes_accessed=12 * m * rank * rank, transcendentals=0),
    )(me, own, got, m1)


def right_kernel(items, a_ref, b_ref, m2_ref, out_ref):
    rows = a_ref.shape[0] // len(items)
    m2 = m2_ref[...]
    sides = (split(m2), split(m2.T))
    for j, (kind, _) in enumerate(items):
        at = pl.ds(j * rows, rows)
        out_ref[at, :] = dot3(split(a_ref[at, :] + b_ref[at, :]), sides[kind])


def right(items, a, b, m2):
    return pl.pallas_call(
        functools.partial(right_kernel, items),
        out_shape=jax.ShapeDtypeStruct(a.shape, jnp.float32),
        in_specs=[VMEM] * 3,
        out_specs=VMEM,
        compiler_params=pltpu.CompilerParams(vmem_limit_bytes=4 << 20),
        name="right",
        cost_estimate=pl.CostEstimate(flops=6 * a.size * a.shape[1], bytes_accessed=12 * a.size, transcendentals=0),
    )(a, b, m2)


def apply_kernel(parts, half, first, last, *refs):
    s_ref, f1_ref, f2t_ref, dirs_ref, res_ref = refs[:5]
    pos = 5
    arrays = []
    for p in parts:
        arrays.append(refs[pos:pos + len(p[4])])
        pos += len(p[4])
    if not first:
        acc_in, prod_in = refs[pos:pos + 2]
        pos += 2
    acc_ref, prod_ref = refs[pos:pos + 2]
    pos += 2
    if last:
        acc_ref, grad_ref = acc_in, acc_ref
    if first:
        f1t_ref = refs[pos]
        pos += 1
        acc_ref[...] = jnp.zeros_like(acc_ref)
        prod_ref[...] = jnp.zeros_like(prod_ref)
    else:
        f1t_ref = f1_ref
        prod_ref[...] = prod_in[...]
    g_ref, r_ref = refs[pos:pos + 2]
    me = s_ref[0]
    core = bit_of(me, 0)
    rank = f2t_ref.shape[0]
    at = 0
    spans = []
    for four in arrays:
        for f in four:
            g_ref[at:at + f.shape[0], :] = f[...].astype(jnp.bfloat16)
            spans.append((at, f.shape[0]))
            at += f.shape[0]

    def tile(k):
        rows = pl.ds(k * TILE, TILE)
        r_ref[k % 2] = jnp.dot(g_ref[...], f2t_ref[:, rows], preferred_element_type=jnp.float32)
        if first:
            f1t_ref[:, rows] = f1_ref[rows, :].astype(jnp.float32).T
        span = iter(spans)
        for items, bits, mode, mine, quarters in parts:
            base = (core if mine else 1 - core) * half
            w = [(res_ref if kind == 0 else dirs_ref)[pl.ds(base + probe, 1), rows] for kind, probe in items]
            prods = [None] * len(items)
            for q in quarters:
                start, _ = next(span)
                sums = {}
                for row, size, r3, j in blocks(len(items), mode, rank):
                    block = r_ref[k % 2, start + row:start + row + size, :]
                    off = pl.multiple_of(offset(me, bits, (q // 2, q % 2) + r3, rank), 32)
                    term = block * w[j]
                    sums[r3] = (off, size, term if r3 not in sums else sums[r3][2] + term)
                    if items[j][0] == 0:
                        p = block * f1t_ref[pl.ds(off, size), rows]
                        p = jnp.sum(p.reshape(size // 8, 8, TILE), axis=0)
                        prods[j] = p if prods[j] is None else prods[j] + p
                for off, size, total in sums.values():
                    acc_ref[pl.ds(off, size), rows] += total
            for (kind, probe), p in zip(items, prods):
                if kind == 0:
                    prod_ref[pl.ds(base + probe, 1), rows] += jnp.sum(p, axis=0, keepdims=True)
        if last:
            grad_ref[rows, :] = acc_ref[:, rows].T

    for k in range(f2t_ref.shape[1] // TILE):
        tile(k)


def apply_cores(parts, half, me, f1, f2t, dirs, res, state, last):
    rank, n = f2t.shape
    first = state is None
    arrays = [a for p in parts for a in p[4].values()]
    shapes = [p[:4] + (tuple(p[4]),) for p in parts]
    total = sum(a.shape[0] for a in arrays)
    ops = [me, f1, f2t, dirs, res] + arrays + ([] if first else list(state))
    acc = jax.ShapeDtypeStruct((n, rank) if last else (rank, n), jnp.float32)
    outs = [acc, jax.ShapeDtypeStruct(dirs.shape, jnp.float32)]
    aliases = {}
    if first:
        outs.append(jax.ShapeDtypeStruct((rank, n), jnp.float32))
    else:
        aliases = {len(ops) - 1: 1}
        if not last:
            aliases[len(ops) - 2] = 0
    return pl.pallas_call(
        functools.partial(apply_kernel, shapes, half, first, last),
        out_shape=outs,
        in_specs=[SMEM] + [VMEM] * (len(ops) - 1),
        out_specs=[VMEM] * len(outs),
        scratch_shapes=[pltpu.VMEM((total, rank), jnp.bfloat16), pltpu.VMEM((2, total, TILE), jnp.float32)],
        input_output_aliases=aliases,
        compiler_params=pltpu.CompilerParams(vmem_limit_bytes=16 << 20),
        name="apply_last" if last else "apply",
        cost_estimate=pl.CostEstimate(flops=2 * total * n * rank, bytes_accessed=8 * n * rank, transcendentals=0),
    )(*ops)


def shards(count, factor_one, factor_two, middle_one, middle_two, directions, residual):
    half = directions.shape[0] // 2
    extra = tuple(range(5, count.bit_length() - 1))

    def swap(x, bit):
        return lax.ppermute(x, AXES, [(i, i ^ (1 << bit)) for i in range(count)])

    me = (lax.axis_index("rows") * lax.axis_size("cores") + lax.axis_index("cores")).astype(jnp.int32).reshape(1)
    items = [(j % 2, j // 2) for j in range(2 * half)]
    groups = []
    at = 0
    for i, (size, bits, mode) in enumerate(GROUPS):
        size = len(items) - at if i == len(GROUPS) - 1 else size
        groups.append((tuple(items[at:at + size]), bits, mode))
        at += size

    other, f1, f2t, dirs, res = open_build(groups[0][0], half, me, factor_one, factor_two, directions, residual)
    args = (me, f1, f2t, dirs, res)
    others = [swap(other, 0)]
    q, after = [], None
    for g, (its, bits, mode) in enumerate(groups):
        own = build(its, True, half, after, *args)
        if g + 1 < len(groups):
            other = build(groups[g + 1][0], False, half, own, *args)
            others.append(swap(other, 0))
        q.append(left(its, bits, mode, me, own, others[g], middle_one))
        after = q[-1][3]
    t = [{} for _ in groups]
    for (_, bits, mode), v, x in zip(groups, t, q):
        v["r11"] = swap(x[3], bits[0])
    for (_, bits, mode), v, x in zip(groups, t, q):
        v["r10"] = swap(x[2], bits[0])
    for (_, bits, mode), v, x in zip(groups, t, q):
        v["r01"] = swap(x[1] + v["r11"], bits[1])
    for (_, bits, mode), v, x in zip(groups, t, q):
        a, b, c = x[0], v["r10"], v["r01"]
        if mode == "h":
            h = a.shape[0] // 2
            v["k"] = (a[:h] + b[:h]) + c[:h]
            v["s"] = (a[h:] + b[h:]) + c[h:]
        else:
            v["s"] = v["k"] = (a + b) + c
        v["r3"] = swap(v["s"], bits[2])
    for (_, bits, mode), v in zip(groups, t):
        v["k"] = v["k"] + v["r3"]
        v["r4"] = swap(v["k"], bits[3])
    for bit in extra:
        for v in t:
            v["k"] = v["k"] + v["r4"]
            v["r4"] = swap(v["k"], bit)
    for (its, bits, mode), v in zip(groups, t):
        v["k"] = right(its, v["k"], v["r4"], middle_two)
        if mode == "h":
            v["k"] = jnp.concatenate([v["k"], swap(v["k"], bits[2])])
    for (_, bits, mode), v in zip(groups, t):
        v["f"] = {0: v["k"]}
        v["f"][1] = swap(v["k"], bits[1])
        v["f"][2] = swap(v["k"], bits[0])
    for (_, bits, mode), v in zip(groups, t):
        v["f"][3] = swap(v["f"][1], bits[0])
        v["o"] = {}
        for i in range(4):
            v["o"][i] = swap(v["f"][i], 0)
    state = None
    for i, stage in enumerate(STAGES):
        parts = []
        for mine in (True, False):
            for (its, bits, mode), v in zip(groups, t):
                arrays = v["f" if mine else "o"]
                parts.append((its, bits, mode, mine, {j: arrays[j] for j in stage}))
        state = apply_cores(
            parts, half, me, f1, f2t, dirs, res, state, i == len(STAGES) - 1
        )
        if i == 0:
            f1, state = state[2], state[:2]
    gradient, products = state
    return products, gradient


def whole(count, *args):
    return shards(count, *args)


def solution(mesh):
    placed = (
        P(AXES, None),
        P(AXES, None),
        P(),
        P(),
        P(None, AXES),
        P(None, AXES),
    )
    count = mesh.shape["rows"] * mesh.shape["cores"]
    return jax.shard_map(
        functools.partial(whole, count),
        mesh=mesh,
        in_specs=placed,
        out_specs=(P(None, AXES), P(AXES, None)),
        check_vma=False,
    )
```

profile of v0, /device:TPU:0, one launch (start us, length us, event | category | flops | bytes accessed | tf_op | source)
XLA Modules:
  0.0 83.1 jit_solution(1675336498186921859)
XLA Ops:
  0.6 3.4 %cores_open.1 = (f32[768,256]{1,0:T(8,128)S(1)}, bf16[2048,256]{1,0:T(8,128)(2,1)S(1)}, bf16[256,2048]{1,0:T(8,128)(2,1)S(1)}, f32[8,2048]{1,0:T(8,128)S(1)}, f32[8,2048]{1,0:T(8,128)S(1)}) custom-call(s32[1]{0:T(128)} %bitcast.s_ref.refs_0_, bf16[2048,256]{1,0:T(8,128)(2,1)} %f1_in.1, bf16[2048,256]{1,0:T(8,128)(2,1)} %f2_in.1, f32[8,2048]{1,0:T(8,128)} %dirs_in.1, ...), custom_call_target="tpu_custom_call" | custom-call | flops 805306368 | bytes 2097152 | tf_op jit(solution)/shard_map/cores_open/pallas_call | solution.py:99
  4.0 0.6 collective-permute-start
  4.6 1.0 %shard_map.77.a_ref.refs_0_ = f32[768,256]{1,0:T(8,128)S(1)} custom-call(s32[1]{0:T(128)} %bitcast.s_ref.refs_0_, bf16[2048,256]{1,0:T(8,128)(2,1)S(1)} %get-tuple-element.26.f1_ref.refs_1_, bf16[256,2048]{1,0:T(8,128)(2,1)S(1)} %get-tuple-element.27.f2t_ref.refs_2_, f32[8,2048]{1,0:T(8,128)S(1)} %get-tuple-element.28.dirs_ref.refs_3_, ...), custom_call_target="tpu_custom_call" | custom-call | flops 805306368 | bytes 2097152 | tf_op jit(solution)/shard_map/pallas_call | solution.py:135
  5.6 1.0 %shard_map.79 = f32[768,256]{1,0:T(8,128)S(1)} custom-call(s32[1]{0:T(128)} %bitcast.s_ref.refs_0_, bf16[2048,256]{1,0:T(8,128)(2,1)S(1)} %get-tuple-element.26.f1_ref.refs_1_, bf16[256,2048]{1,0:T(8,128)(2,1)S(1)} %get-tuple-element.27.f2t_ref.refs_2_, f32[8,2048]{1,0:T(8,128)S(1)} %get-tuple-element.28.dirs_ref.refs_3_, ...), custom_call_target="tpu_custom_call" | custom-call | flops 805306368 | bytes 2097152 | tf_op jit(solution)/shard_map/pallas_call | solution.py:135
  6.7 0.6 left.3
  7.3 1.0 %shard_map.78.a_ref.refs_0_ = f32[768,256]{1,0:T(8,128)S(1)} custom-call(s32[1]{0:T(128)} %bitcast.s_ref.refs_0_, bf16[2048,256]{1,0:T(8,128)(2,1)S(1)} %get-tuple-element.26.f1_ref.refs_1_, bf16[256,2048]{1,0:T(8,128)(2,1)S(1)} %get-tuple-element.27.f2t_ref.refs_2_, f32[8,2048]{1,0:T(8,128)S(1)} %get-tuple-element.28.dirs_ref.refs_3_, ...), custom_call_target="tpu_custom_call" | custom-call | flops 805306368 | bytes 2097152 | tf_op jit(solution)/shard_map/pallas_call | solution.py:135
  8.3 0.7 collective-permute-done.7.b_ref
  8.9 0.6 left.4
  9.5 2.7 %collective-permute-start.9 = (f32[192,256]{1,0:T(8,128)S(1)}, f32[192,256]{1,0:T(8,128)S(1)}, u32[]{:S(2)}, u32[]{:S(2)}) collective-permute-start(f32[192,256]{1,0:T(8,128)S(1)} %get-tuple-element.38.refs_0_), channel_id=1, source_target_pairs={{0,2},{1,3},{2,0},{3,1},{4,6},{5,7},{6,4},{7,5},{8,10},{9,11},{10,... | collective-permute-start | bytes 589832 | tf_op jit(solution)/shard_map/ppermute | solution.py:300
  12.2 1.5 %collective-permute-start.2 = (f32[192,256]{1,0:T(8,128)S(1)}, f32[192,256]{1,0:T(8,128)S(1)}, u32[]{:S(2)}, u32[]{:S(2)}) collective-permute-start(f32[192,256]{1,0:T(8,128)S(1)} %get-tuple-element.34.refs_0_), channel_id=1, source_target_pairs={{0,4},{1,5},{2,6},{3,7},{4,0},{5,1},{6,2},{7,3},{8,12},{9,13},{10,... | collective-permute-start | bytes 589832 | tf_op jit(solution)/shard_map/ppermute | solution.py:300
  13.7 0.5 collective-permute-start.8
  14.2 3.8 %collective-permute-done.9 = f32[192,256]{1,0:T(8,128)S(1)} collective-permute-done((f32[192,256]{1,0:T(8,128)S(1)}, f32[192,256]{1,0:T(8,128)S(1)}, u32[]{:S(2)}, u32[]{:S(2)}) %collective-permute-start.9) | collective-permute-done | bytes 196640 | tf_op jit(solution)/shard_map/ppermute | solution.py:300
  18.0 2.1 %collective-permute-start.10 = (f32[192,256]{1,0:T(8,128)S(1)}, f32[192,256]{1,0:T(8,128)S(1)}, u32[]{:S(2)}, u32[]{:S(2)}) collective-permute-start(f32[192,256]{1,0:T(8,128)S(1)} %add.59), channel_id=1, source_target_pairs={{0,8},{1,9},{2,10},{3,11},{4,12},{5,13},{6,14},{7,15},{8,0},{9,1},... | collective-permute-start | bytes 589832 | tf_op jit(solution)/shard_map/ppermute | solution.py:300
  20.2 0.7 shard_map.81
  21.0 1.6 %collective-permute-start.1 = (f32[192,256]{1,0:T(8,128)S(1)}, f32[192,256]{1,0:T(8,128)S(1)}, u32[]{:S(2)}, u32[]{:S(2)}) collective-permute-start(f32[192,256]{1,0:T(8,128)S(1)} %get-tuple-element.32), channel_id=1, source_target_pairs={{0,4},{1,5},{2,6},{3,7},{4,0},{5,1},{6,2},{7,3},{8,12},{9,13},{10,... | collective-permute-start | bytes 589832 | tf_op jit(solution)/shard_map/ppermute | solution.py:300
  22.5 0.7 shard_map.80.a_ref
  23.3 1.6 %collective-permute-start.3 = (f32[192,256]{1,0:T(8,128)S(1)}, f32[192,256]{1,0:T(8,128)S(1)}, u32[]{:S(2)}, u32[]{:S(2)}) collective-permute-start(f32[192,256]{1,0:T(8,128)S(1)} %add.53), channel_id=1, source_target_pairs={{0,2},{1,3},{2,0},{3,1},{4,6},{5,7},{6,4},{7,5},{8,10},{9,11},{10,... | collective-permute-start | bytes 589832 | tf_op jit(solution)/shard_map/ppermute | solution.py:300
  24.9 1.0 %collective-permute-start.11 = (f32[96,256]{1,0:T(8,128)S(1)}, f32[96,256]{1,0:T(8,128)S(1)}, u32[]{:S(2)}, u32[]{:S(2)}) collective-permute-start(f32[96,256]{1,0:T(8,128)S(1)} %slice_add_fusion), channel_id=1, source_target_pairs={{0,4},{1,5},{2,6},{3,7},{4,0},{5,1},{6,2},{7,3},{8,12},{9,13},{10,... | collective-permute-start | bytes 294920 | tf_op jit(solution)/shard_map/ppermute | solution.py:300
  25.9 2.9 %collective-permute-done.1 = f32[192,256]{1,0:T(8,128)S(1)} collective-permute-done((f32[192,256]{1,0:T(8,128)S(1)}, f32[192,256]{1,0:T(8,128)S(1)}, u32[]{:S(2)}, u32[]{:S(2)}) %collective-permute-start.1) | collective-permute-done | bytes 196640 | tf_op jit(solution)/shard_map/ppermute | solution.py:300
  28.8 1.5 %collective-permute-done.3 = f32[192,256]{1,0:T(8,128)S(1)} collective-permute-done((f32[192,256]{1,0:T(8,128)S(1)}, f32[192,256]{1,0:T(8,128)S(1)}, u32[]{:S(2)}, u32[]{:S(2)}) %collective-permute-start.3) | collective-permute-done | bytes 196640 | tf_op jit(solution)/shard_map/ppermute | solution.py:300
  30.4 0.5 collective-permute-start.4
  30.9 2.7 %collective-permute-start.12 = (f32[96,256]{1,0:T(8,128)S(1)}, f32[96,256]{1,0:T(8,128)S(1)}, u32[]{:S(2)}, u32[]{:S(2)}) collective-permute-start(f32[96,256]{1,0:T(8,128)S(1)} %fusion.a_ref), channel_id=1, source_target_pairs={{0,16},{1,17},{2,18},{3,19},{4,20},{5,21},{6,22},{7,23},{8,24},{9,... | collective-permute-start | bytes 294920 | tf_op jit(solution)/shard_map/ppermute | solution.py:300
  34.0 1.6 %collective-permute-start.16 = (f32[128,256]{1,0:T(8,128)S(1)}, f32[128,256]{1,0:T(8,128)S(1)}, u32[]{:S(2)}, u32[]{:S(2)}) collective-permute-start(f32[128,256]{1,0:T(8,128)S(1)} %get-tuple-element.42), channel_id=1, source_target_pairs={{0,8},{1,9},{2,10},{3,11},{4,12},{5,13},{6,14},{7,15},{8,0},{9,1},... | collective-permute-start | bytes 393224 | tf_op jit(solution)/shard_map/ppermute | solution.py:300
  35.9 2.9 %collective-permute-start.5 = (f32[96,256]{1,0:T(8,128)S(1)}, f32[96,256]{1,0:T(8,128)S(1)}, u32[]{:S(2)}, u32[]{:S(2)}) collective-permute-start(f32[96,256]{1,0:T(8,128)S(1)} %fusion.1.a_ref), channel_id=1, source_target_pairs={{0,16},{1,17},{2,18},{3,19},{4,20},{5,21},{6,22},{7,23},{8,24},{9,... | collective-permute-start | bytes 294920 | tf_op jit(solution)/shard_map/ppermute | solution.py:300
  38.8 0.5 right.4
  39.3 0.6 collective-permute-start.13
  39.9 2.0 %collective-permute-start.15 = (f32[128,256]{1,0:T(8,128)S(1)}, f32[128,256]{1,0:T(8,128)S(1)}, u32[]{:S(2)}, u32[]{:S(2)}) collective-permute-start(f32[128,256]{1,0:T(8,128)S(1)} %get-tuple-element.40), channel_id=1, source_target_pairs={{0,8},{1,9},{2,10},{3,11},{4,12},{5,13},{6,14},{7,15},{8,0},{9,1},... | collective-permute-start | bytes 393224 | tf_op jit(solution)/shard_map/ppermute | solution.py:300
  41.9 1.6 %collective-permute-start.17 = (f32[128,256]{1,0:T(8,128)S(1)}, f32[128,256]{1,0:T(8,128)S(1)}, u32[]{:S(2)}, u32[]{:S(2)}) collective-permute-start(f32[128,256]{1,0:T(8,128)S(1)} %add.65), channel_id=1, source_target_pairs={{0,4},{1,5},{2,6},{3,7},{4,0},{5,1},{6,2},{7,3},{8,12},{9,13},{10,... | collective-permute-start | bytes 393224 | tf_op jit(solution)/shard_map/ppermute | solution.py:300
  43.5 0.5 right.3
  43.9 2.0 %collective-permute-start.6 = (f32[96,256]{1,0:T(8,128)S(1)}, f32[96,256]{1,0:T(8,128)S(1)}, u32[]{:S(2)}, u32[]{:S(2)}) collective-permute-start(f32[96,256]{1,0:T(8,128)S(1)} %right.3), channel_id=1, source_target_pairs={{0,8},{1,9},{2,10},{3,11},{4,12},{5,13},{6,14},{7,15},{8,0},{9,1},... | collective-permute-start | bytes 294920 | tf_op jit(solution)/shard_map/ppermute | solution.py:300
  46.2 1.5 %collective-permute-start.33 = (f32[192,256]{1,0:T(8,128)S(1)}, f32[192,256]{1,0:T(8,128)S(1)}, u32[]{:S(2)}, u32[]{:S(2)}) collective-permute-start(f32[192,256]{1,0:T(8,128)S(1)} %pad_maximum_fusion.1.refs_6_), channel_id=1, source_target_pairs={{0,2},{1,3},{2,0},{3,1},{4,6},{5,7},{6,4},{7,5},{8,10},{9,11},{10,... | collective-permute-start | bytes 589832 | tf_op jit(solution)/shard_map/ppermute | solution.py:300
  47.7 2.6 %collective-permute-start.18 = (f32[128,256]{1,0:T(8,128)S(1)}, f32[128,256]{1,0:T(8,128)S(1)}, u32[]{:S(2)}, u32[]{:S(2)}) collective-permute-start(f32[128,256]{1,0:T(8,128)S(1)} %add_add_fusion), channel_id=1, source_target_pairs={{0,16},{1,17},{2,18},{3,19},{4,20},{5,21},{6,22},{7,23},{8,24},{9,... | collective-permute-start | bytes 393224 | tf_op jit(solution)/shard_map/ppermute | solution.py:300
  50.3 1.0 %collective-permute-start.23 = (f32[192,256]{1,0:T(8,128)S(1)}, f32[192,256]{1,0:T(8,128)S(1)}, u32[]{:S(2)}, u32[]{:S(2)}) collective-permute-start(f32[192,256]{1,0:T(8,128)S(1)} %pad_maximum_fusion.refs_5_), channel_id=1, source_target_pairs={{0,2},{1,3},{2,0},{3,1},{4,6},{5,7},{6,4},{7,5},{8,10},{9,11},{10,... | collective-permute-start | bytes 589832 | tf_op jit(solution)/shard_map/ppermute | solution.py:300
  51.4 3.6 %collective-permute-done.18 = f32[128,256]{1,0:T(8,128)S(1)} collective-permute-done((f32[128,256]{1,0:T(8,128)S(1)}, f32[128,256]{1,0:T(8,128)S(1)}, u32[]{:S(2)}, u32[]{:S(2)}) %collective-permute-start.18) | collective-permute-done | bytes 131104 | tf_op jit(solution)/shard_map/ppermute | solution.py:300
  55.3 1.6 %collective-permute-start.19 = (f32[128,256]{1,0:T(8,128)S(1)}, f32[128,256]{1,0:T(8,128)S(1)}, u32[]{:S(2)}, u32[]{:S(2)}) collective-permute-start(f32[128,256]{1,0:T(8,128)S(1)} %add.67.a_ref), channel_id=1, source_target_pairs={{0,2},{1,3},{2,0},{3,1},{4,6},{5,7},{6,4},{7,5},{8,10},{9,11},{10,... | collective-permute-start | bytes 393224 | tf_op jit(solution)/shard_map/ppermute | solution.py:300
  56.9 0.5 collective-permute-start.37
  57.4 0.8 collective-permute-done.23.refs_5_
  58.2 2.6 %collective-permute-done.32.refs_6_ = f32[192,256]{1,0:T(8,128)S(1)} collective-permute-done((f32[192,256]{1,0:T(8,128)S(1)}, f32[192,256]{1,0:T(8,128)S(1)}, u32[]{:S(2)}, u32[]{:S(2)}) %collective-permute-start.32) | collective-permute-done | bytes 196640 | tf_op jit(solution)/shard_map/ppermute | solution.py:300
  60.8 0.5 collective-permute-start.36
  61.7 0.9 %collective-permute-start.27 = (f32[128,256]{1,0:T(8,128)S(1)}, f32[128,256]{1,0:T(8,128)S(1)}, u32[]{:S(2)}, u32[]{:S(2)}) collective-permute-start(f32[128,256]{1,0:T(8,128)S(1)} %right.5.refs_7_), channel_id=1, source_target_pairs={{0,4},{1,5},{2,6},{3,7},{4,0},{5,1},{6,2},{7,3},{8,12},{9,13},{10,... | collective-permute-start | bytes 393224 | tf_op jit(solution)/shard_map/ppermute | solution.py:300
  62.8 3.1 %collective-permute-start.34 = (f32[128,256]{1,0:T(8,128)S(1)}, f32[128,256]{1,0:T(8,128)S(1)}, u32[]{:S(2)}, u32[]{:S(2)}) collective-permute-start(f32[128,256]{1,0:T(8,128)S(1)} %right.5.refs_7_), channel_id=1, source_target_pairs={{0,8},{1,9},{2,10},{3,11},{4,12},{5,13},{6,14},{7,15},{8,0},{9,1},... | collective-permute-start | bytes 393224 | tf_op jit(solution)/shard_map/ppermute | solution.py:300
  66.0 1.5 %collective-permute-start.26 = (f32[192,256]{1,0:T(8,128)S(1)}, f32[192,256]{1,0:T(8,128)S(1)}, u32[]{:S(2)}, u32[]{:S(2)}) collective-permute-start(f32[192,256]{1,0:T(8,128)S(1)} %collective-permute-done.25.refs_7_), channel_id=1, source_target_pairs={{0,2},{1,3},{2,0},{3,1},{4,6},{5,7},{6,4},{7,5},{8,10},{9,11},{10,... | collective-permute-start | bytes 589832 | tf_op jit(solution)/shard_map/ppermute | solution.py:300
  67.5 1.0 %collective-permute-start.24 = (f32[192,256]{1,0:T(8,128)S(1)}, f32[192,256]{1,0:T(8,128)S(1)}, u32[]{:S(2)}, u32[]{:S(2)}) collective-permute-start(f32[192,256]{1,0:T(8,128)S(1)} %collective-permute-done.23.refs_5_), channel_id=1, source_target_pairs={{0,4},{1,5},{2,6},{3,7},{4,0},{5,1},{6,2},{7,3},{8,12},{9,13},{10,... | collective-permute-start | bytes 589832 | tf_op jit(solution)/shard_map/ppermute | solution.py:300
  68.5 1.9 %collective-permute-start.28 = (f32[128,256]{1,0:T(8,128)S(1)}, f32[128,256]{1,0:T(8,128)S(1)}, u32[]{:S(2)}, u32[]{:S(2)}) collective-permute-start(f32[128,256]{1,0:T(8,128)S(1)} %collective-permute-done.27.refs_9_), channel_id=1, source_target_pairs={{0,8},{1,9},{2,10},{3,11},{4,12},{5,13},{6,14},{7,15},{8,0},{9,1},... | collective-permute-start | bytes 393224 | tf_op jit(solution)/shard_map/ppermute | solution.py:300
  70.4 0.5 collective-permute-start.40
  70.9 2.8 %apply.2 = (f32[256,2048]{1,0:T(8,128)S(1)}, f32[8,2048]{1,0:T(8,128)}, f32[256,2048]{1,0:T(8,128)S(1)}) custom-call(s32[1]{0:T(128)} %bitcast.s_ref.refs_0_, bf16[2048,256]{1,0:T(8,128)(2,1)S(1)} %get-tuple-element.26.f1_ref.refs_1_, bf16[256,2048]{1,0:T(8,128)(2,1)S(1)} %get-tuple-element.27.f2t_ref.refs_2_, ...), custom_call_target="tpu_custom_call" | custom-call | flops 1073741824 | bytes 4194304 | tf_op jit(solution)/shard_map/apply/pallas_call | solution.py:282
  74.7 4.3 %apply.3 = (f32[256,2048]{1,0:T(8,128)S(1)}, f32[8,2048]{1,0:T(8,128)}) custom-call(s32[1]{0:T(128)} %bitcast.s_ref.refs_0_, f32[256,2048]{1,0:T(8,128)S(1)} %get-tuple-element.43.refs_1_, bf16[256,2048]{1,0:T(8,128)(2,1)S(1)} %get-tuple-element.27.f2t_ref.refs_2_, ...), custom_call_target="tpu_custom_call", output_to_operand_aliasing={{1}: (18, {}), {0}: (17, {})} | custom-call | flops 2147483648 | bytes 4194304 | tf_op jit(solution)/shard_map/apply/pallas_call | solution.py:282
  79.0 4.1 %apply_last.1 = (f32[2048,256]{1,0:T(8,128)}, f32[8,2048]{1,0:T(8,128)}) custom-call(s32[1]{0:T(128)} %bitcast.s_ref.refs_0_, f32[256,2048]{1,0:T(8,128)S(1)} %get-tuple-element.43.refs_1_, bf16[256,2048]{1,0:T(8,128)(2,1)S(1)} %get-tuple-element.27.f2t_ref.refs_2_, ...), custom_call_target="tpu_custom_call", output_to_operand_aliasing={{1}: (12, {})} | custom-call | flops 1073741824 | bytes 4194304 | tf_op jit(solution)/shard_map/apply_last/pallas_call | solution.py:282
  (64 shorter events, 3.1 us)
Async XLA Ops:
  4.0 2.6 %collective-permute-start = (f32[768,256]{1,0:T(8,128)S(1)}, f32[768,256]{1,0:T(8,128)S(1)}, u32[]{:S(2)}, u32[]{:S(2)}) collective-permute-start(f32[768,256]{1,0:T(8,128)S(1)} %get-tuple-element.30), channel_id=1, source_target_pairs={{0,1},{1,0},{2,3},{3,2},{4,5},{5,4},{6,7},{7,6},{8,9},{9,8},{10,11... | collective-permute-start | bytes 2359304 | tf_op jit(solution)/shard_map/ppermute | solution.py:300
  5.6 1.1 %copy-start.1 = (f32[256,256]{1,0:T(8,128)S(1)}, f32[256,256]{1,0:T(8,128)}, u32[]{:S(2)}) copy-start(f32[256,256]{1,0:T(8,128)} %m1_ref.5) | copy-start | bytes 786436
  6.6 2.4 %collective-permute-start.7 = (f32[768,256]{1,0:T(8,128)S(1)}, f32[768,256]{1,0:T(8,128)S(1)}, u32[]{:S(2)}, u32[]{:S(2)}) collective-permute-start(f32[768,256]{1,0:T(8,128)S(1)} %shard_map.79), channel_id=1, source_target_pairs={{0,1},{1,0},{2,3},{3,2},{4,5},{5,4},{6,7},{7,6},{8,9},{9,8},{10,11... | collective-permute-start | bytes 2359304 | tf_op jit(solution)/shard_map/ppermute | solution.py:300
  9.5 8.5 %collective-permute-start.9 = (f32[192,256]{1,0:T(8,128)S(1)}, f32[192,256]{1,0:T(8,128)S(1)}, u32[]{:S(2)}, u32[]{:S(2)}) collective-permute-start(f32[192,256]{1,0:T(8,128)S(1)} %get-tuple-element.38.refs_0_), channel_id=1, source_target_pairs={{0,2},{1,3},{2,0},{3,1},{4,6},{5,7},{6,4},{7,5},{8,10},{9,11},{10,... | collective-permute-start | bytes 589832 | tf_op jit(solution)/shard_map/ppermute | solution.py:300
  12.2 11.0 %collective-permute-start.2 = (f32[192,256]{1,0:T(8,128)S(1)}, f32[192,256]{1,0:T(8,128)S(1)}, u32[]{:S(2)}, u32[]{:S(2)}) collective-permute-start(f32[192,256]{1,0:T(8,128)S(1)} %get-tuple-element.34.refs_0_), channel_id=1, source_target_pairs={{0,4},{1,5},{2,6},{3,7},{4,0},{5,1},{6,2},{7,3},{8,12},{9,13},{10,... | collective-permute-start | bytes 589832 | tf_op jit(solution)/shard_map/ppermute | solution.py:300
  13.7 11.2 %collective-permute-start.8 = (f32[192,256]{1,0:T(8,128)S(1)}, f32[192,256]{1,0:T(8,128)S(1)}, u32[]{:S(2)}, u32[]{:S(2)}) collective-permute-start(f32[192,256]{1,0:T(8,128)S(1)} %get-tuple-element.36), channel_id=1, source_target_pairs={{0,2},{1,3},{2,0},{3,1},{4,6},{5,7},{6,4},{7,5},{8,10},{9,11},{10,... | collective-permute-start | bytes 589832 | tf_op jit(solution)/shard_map/ppermute | solution.py:300
  18.0 6.9 %collective-permute-start.10 = (f32[192,256]{1,0:T(8,128)S(1)}, f32[192,256]{1,0:T(8,128)S(1)}, u32[]{:S(2)}, u32[]{:S(2)}) collective-permute-start(f32[192,256]{1,0:T(8,128)S(1)} %add.59), channel_id=1, source_target_pairs={{0,8},{1,9},{2,10},{3,11},{4,12},{5,13},{6,14},{7,15},{8,0},{9,1},... | collective-permute-start | bytes 589832 | tf_op jit(solution)/shard_map/ppermute | solution.py:300
  20.9 12.7 %collective-permute-start.14 = (f32[512,256]{1,0:T(8,128)S(1)}, f32[512,256]{1,0:T(8,128)S(1)}, u32[]{:S(2)}, u32[]{:S(2)}) collective-permute-start(f32[512,256]{1,0:T(8,128)S(1)} %shard_map.81), channel_id=1, source_target_pairs={{0,1},{1,0},{2,3},{3,2},{4,5},{5,4},{6,7},{7,6},{8,9},{9,8},{10,11... | collective-permute-start | bytes 1572872 | tf_op jit(solution)/shard_map/ppermute | solution.py:300
  21.0 7.8 %collective-permute-start.1 = (f32[192,256]{1,0:T(8,128)S(1)}, f32[192,256]{1,0:T(8,128)S(1)}, u32[]{:S(2)}, u32[]{:S(2)}) collective-permute-start(f32[192,256]{1,0:T(8,128)S(1)} %get-tuple-element.32), channel_id=1, source_target_pairs={{0,4},{1,5},{2,6},{3,7},{4,0},{5,1},{6,2},{7,3},{8,12},{9,13},{10,... | collective-permute-start | bytes 589832 | tf_op jit(solution)/shard_map/ppermute | solution.py:300
  23.2 15.5 %copy-start = (f32[256,256]{1,0:T(8,128)S(1)}, f32[256,256]{1,0:T(8,128)}, u32[]{:S(2)}) copy-start(f32[256,256]{1,0:T(8,128)} %m2_ref.5) | copy-start | bytes 786436
  23.3 7.0 %collective-permute-start.3 = (f32[192,256]{1,0:T(8,128)S(1)}, f32[192,256]{1,0:T(8,128)S(1)}, u32[]{:S(2)}, u32[]{:S(2)}) collective-permute-start(f32[192,256]{1,0:T(8,128)S(1)} %add.53), channel_id=1, source_target_pairs={{0,2},{1,3},{2,0},{3,1},{4,6},{5,7},{6,4},{7,5},{8,10},{9,11},{10,... | collective-permute-start | bytes 589832 | tf_op jit(solution)/shard_map/ppermute | solution.py:300
  24.9 6.0 %collective-permute-start.11 = (f32[96,256]{1,0:T(8,128)S(1)}, f32[96,256]{1,0:T(8,128)S(1)}, u32[]{:S(2)}, u32[]{:S(2)}) collective-permute-start(f32[96,256]{1,0:T(8,128)S(1)} %slice_add_fusion), channel_id=1, source_target_pairs={{0,4},{1,5},{2,6},{3,7},{4,0},{5,1},{6,2},{7,3},{8,12},{9,13},{10,... | collective-permute-start | bytes 294920 | tf_op jit(solution)/shard_map/ppermute | solution.py:300
  30.4 5.5 %collective-permute-start.4 = (f32[96,256]{1,0:T(8,128)S(1)}, f32[96,256]{1,0:T(8,128)S(1)}, u32[]{:S(2)}, u32[]{:S(2)}) collective-permute-start(f32[96,256]{1,0:T(8,128)S(1)} %slice_add_fusion.4), channel_id=1, source_target_pairs={{0,8},{1,9},{2,10},{3,11},{4,12},{5,13},{6,14},{7,15},{8,0},{9,1},... | collective-permute-start | bytes 294920 | tf_op jit(solution)/shard_map/ppermute | solution.py:300
  30.9 7.9 %collective-permute-start.12 = (f32[96,256]{1,0:T(8,128)S(1)}, f32[96,256]{1,0:T(8,128)S(1)}, u32[]{:S(2)}, u32[]{:S(2)}) collective-permute-start(f32[96,256]{1,0:T(8,128)S(1)} %fusion.a_ref), channel_id=1, source_target_pairs={{0,16},{1,17},{2,18},{3,19},{4,20},{5,21},{6,22},{7,23},{8,24},{9,... | collective-permute-start | bytes 294920 | tf_op jit(solution)/shard_map/ppermute | solution.py:300
  34.0 7.8 %collective-permute-start.16 = (f32[128,256]{1,0:T(8,128)S(1)}, f32[128,256]{1,0:T(8,128)S(1)}, u32[]{:S(2)}, u32[]{:S(2)}) collective-permute-start(f32[128,256]{1,0:T(8,128)S(1)} %get-tuple-element.42), channel_id=1, source_target_pairs={{0,8},{1,9},{2,10},{3,11},{4,12},{5,13},{6,14},{7,15},{8,0},{9,1},... | collective-permute-start | bytes 393224 | tf_op jit(solution)/shard_map/ppermute | solution.py:300
  35.9 7.6 %collective-permute-start.5 = (f32[96,256]{1,0:T(8,128)S(1)}, f32[96,256]{1,0:T(8,128)S(1)}, u32[]{:S(2)}, u32[]{:S(2)}) collective-permute-start(f32[96,256]{1,0:T(8,128)S(1)} %fusion.1.a_ref), channel_id=1, source_target_pairs={{0,16},{1,17},{2,18},{3,19},{4,20},{5,21},{6,22},{7,23},{8,24},{9,... | collective-permute-start | bytes 294920 | tf_op jit(solution)/shard_map/ppermute | solution.py:300
  39.3 6.6 %collective-permute-start.13 = (f32[96,256]{1,0:T(8,128)S(1)}, f32[96,256]{1,0:T(8,128)S(1)}, u32[]{:S(2)}, u32[]{:S(2)}) collective-permute-start(f32[96,256]{1,0:T(8,128)S(1)} %right.4), channel_id=1, source_target_pairs={{0,4},{1,5},{2,6},{3,7},{4,0},{5,1},{6,2},{7,3},{8,12},{9,13},{10,... | collective-permute-start | bytes 294920 | tf_op jit(solution)/shard_map/ppermute | solution.py:300
  39.9 6.3 %collective-permute-start.15 = (f32[128,256]{1,0:T(8,128)S(1)}, f32[128,256]{1,0:T(8,128)S(1)}, u32[]{:S(2)}, u32[]{:S(2)}) collective-permute-start(f32[128,256]{1,0:T(8,128)S(1)} %get-tuple-element.40), channel_id=1, source_target_pairs={{0,8},{1,9},{2,10},{3,11},{4,12},{5,13},{6,14},{7,15},{8,0},{9,1},... | collective-permute-start | bytes 393224 | tf_op jit(solution)/shard_map/ppermute | solution.py:300
  41.9 5.8 %collective-permute-start.17 = (f32[128,256]{1,0:T(8,128)S(1)}, f32[128,256]{1,0:T(8,128)S(1)}, u32[]{:S(2)}, u32[]{:S(2)}) collective-permute-start(f32[128,256]{1,0:T(8,128)S(1)} %add.65), channel_id=1, source_target_pairs={{0,4},{1,5},{2,6},{3,7},{4,0},{5,1},{6,2},{7,3},{8,12},{9,13},{10,... | collective-permute-start | bytes 393224 | tf_op jit(solution)/shard_map/ppermute | solution.py:300
  43.9 6.4 %collective-permute-start.6 = (f32[96,256]{1,0:T(8,128)S(1)}, f32[96,256]{1,0:T(8,128)S(1)}, u32[]{:S(2)}, u32[]{:S(2)}) collective-permute-start(f32[96,256]{1,0:T(8,128)S(1)} %right.3), channel_id=1, source_target_pairs={{0,8},{1,9},{2,10},{3,11},{4,12},{5,13},{6,14},{7,15},{8,0},{9,1},... | collective-permute-start | bytes 294920 | tf_op jit(solution)/shard_map/ppermute | solution.py:300
  45.9 9.3 %collective-permute-start.21 = (f32[192,256]{1,0:T(8,128)S(1)}, f32[192,256]{1,0:T(8,128)S(1)}, u32[]{:S(2)}, u32[]{:S(2)}) collective-permute-start(f32[192,256]{1,0:T(8,128)S(1)} %pad_maximum_fusion.1.refs_6_), channel_id=1, source_target_pairs={{0,1},{1,0},{2,3},{3,2},{4,5},{5,4},{6,7},{7,6},{8,9},{9,8},{10,11... | collective-permute-start | bytes 589832 | tf_op jit(solution)/shard_map/ppermute | solution.py:300
  46.0 10.8 %collective-permute-start.25 = (f32[192,256]{1,0:T(8,128)S(1)}, f32[192,256]{1,0:T(8,128)S(1)}, u32[]{:S(2)}, u32[]{:S(2)}) collective-permute-start(f32[192,256]{1,0:T(8,128)S(1)} %pad_maximum_fusion.1.refs_6_), channel_id=1, source_target_pairs={{0,8},{1,9},{2,10},{3,11},{4,12},{5,13},{6,14},{7,15},{8,0},{9,1},... | collective-permute-start | bytes 589832 | tf_op jit(solution)/shard_map/ppermute | solution.py:300
  46.2 10.7 %collective-permute-start.33 = (f32[192,256]{1,0:T(8,128)S(1)}, f32[192,256]{1,0:T(8,128)S(1)}, u32[]{:S(2)}, u32[]{:S(2)}) collective-permute-start(f32[192,256]{1,0:T(8,128)S(1)} %pad_maximum_fusion.1.refs_6_), channel_id=1, source_target_pairs={{0,2},{1,3},{2,0},{3,1},{4,6},{5,7},{6,4},{7,5},{8,10},{9,11},{10,... | collective-permute-start | bytes 589832 | tf_op jit(solution)/shard_map/ppermute | solution.py:300
  47.7 7.3 %collective-permute-start.18 = (f32[128,256]{1,0:T(8,128)S(1)}, f32[128,256]{1,0:T(8,128)S(1)}, u32[]{:S(2)}, u32[]{:S(2)}) collective-permute-start(f32[128,256]{1,0:T(8,128)S(1)} %add_add_fusion), channel_id=1, source_target_pairs={{0,16},{1,17},{2,18},{3,19},{4,20},{5,21},{6,22},{7,23},{8,24},{9,... | collective-permute-start | bytes 393224 | tf_op jit(solution)/shard_map/ppermute | solution.py:300
  50.3 7.8 %collective-permute-start.23 = (f32[192,256]{1,0:T(8,128)S(1)}, f32[192,256]{1,0:T(8,128)S(1)}, u32[]{:S(2)}, u32[]{:S(2)}) collective-permute-start(f32[192,256]{1,0:T(8,128)S(1)} %pad_maximum_fusion.refs_5_), channel_id=1, source_target_pairs={{0,2},{1,3},{2,0},{3,1},{4,6},{5,7},{6,4},{7,5},{8,10},{9,11},{10,... | collective-permute-start | bytes 589832 | tf_op jit(solution)/shard_map/ppermute | solution.py:300
  55.0 5.8 %collective-permute-start.32 = (f32[192,256]{1,0:T(8,128)S(1)}, f32[192,256]{1,0:T(8,128)S(1)}, u32[]{:S(2)}, u32[]{:S(2)}) collective-permute-start(f32[192,256]{1,0:T(8,128)S(1)} %pad_maximum_fusion.refs_5_), channel_id=1, source_target_pairs={{0,4},{1,5},{2,6},{3,7},{4,0},{5,1},{6,2},{7,3},{8,12},{9,13},{10,... | collective-permute-start | bytes 589832 | tf_op jit(solution)/shard_map/ppermute | solution.py:300
  55.3 5.5 %collective-permute-start.19 = (f32[128,256]{1,0:T(8,128)S(1)}, f32[128,256]{1,0:T(8,128)S(1)}, u32[]{:S(2)}, u32[]{:S(2)}) collective-permute-start(f32[128,256]{1,0:T(8,128)S(1)} %add.67.a_ref), channel_id=1, source_target_pairs={{0,2},{1,3},{2,0},{3,1},{4,6},{5,7},{6,4},{7,5},{8,10},{9,11},{10,... | collective-permute-start | bytes 393224 | tf_op jit(solution)/shard_map/ppermute | solution.py:300
  56.8 4.9 %collective-permute-start.20 = (f32[192,256]{1,0:T(8,128)S(1)}, f32[192,256]{1,0:T(8,128)S(1)}, u32[]{:S(2)}, u32[]{:S(2)}) collective-permute-start(f32[192,256]{1,0:T(8,128)S(1)} %pad_maximum_fusion.refs_5_), channel_id=1, source_target_pairs={{0,1},{1,0},{2,3},{3,2},{4,5},{5,4},{6,7},{7,6},{8,9},{9,8},{10,11... | collective-permute-start | bytes 589832 | tf_op jit(solution)/shard_map/ppermute | solution.py:300
  56.9 5.7 %collective-permute-start.37 = (f32[192,256]{1,0:T(8,128)S(1)}, f32[192,256]{1,0:T(8,128)S(1)}, u32[]{:S(2)}, u32[]{:S(2)}) collective-permute-start(f32[192,256]{1,0:T(8,128)S(1)} %collective-permute-done.25.refs_7_), channel_id=1, source_target_pairs={{0,1},{1,0},{2,3},{3,2},{4,5},{5,4},{6,7},{7,6},{8,9},{9,8},{10,11... | collective-permute-start | bytes 589832 | tf_op jit(solution)/shard_map/ppermute | solution.py:300
  58.2 4.6 %collective-permute-start.38 = (f32[192,256]{1,0:T(8,128)S(1)}, f32[192,256]{1,0:T(8,128)S(1)}, u32[]{:S(2)}, u32[]{:S(2)}) collective-permute-start(f32[192,256]{1,0:T(8,128)S(1)} %collective-permute-done.33.refs_8_), channel_id=1, source_target_pairs={{0,1},{1,0},{2,3},{3,2},{4,5},{5,4},{6,7},{7,6},{8,9},{9,8},{10,11... | collective-permute-start | bytes 589832 | tf_op jit(solution)/shard_map/ppermute | solution.py:300
  60.8 5.2 %collective-permute-start.35 = (f32[192,256]{1,0:T(8,128)S(1)}, f32[192,256]{1,0:T(8,128)S(1)}, u32[]{:S(2)}, u32[]{:S(2)}) collective-permute-start(f32[192,256]{1,0:T(8,128)S(1)} %collective-permute-done.23.refs_5_), channel_id=1, source_target_pairs={{0,1},{1,0},{2,3},{3,2},{4,5},{5,4},{6,7},{7,6},{8,9},{9,8},{10,11... | collective-permute-start | bytes 589832 | tf_op jit(solution)/shard_map/ppermute | solution.py:300
  60.8 6.7 %collective-permute-start.36 = (f32[192,256]{1,0:T(8,128)S(1)}, f32[192,256]{1,0:T(8,128)S(1)}, u32[]{:S(2)}, u32[]{:S(2)}) collective-permute-start(f32[192,256]{1,0:T(8,128)S(1)} %collective-permute-done.32.refs_6_), channel_id=1, source_target_pairs={{0,1},{1,0},{2,3},{3,2},{4,5},{5,4},{6,7},{7,6},{8,9},{9,8},{10,11... | collective-permute-start | bytes 589832 | tf_op jit(solution)/shard_map/ppermute | solution.py:300
  61.7 6.8 %collective-permute-start.27 = (f32[128,256]{1,0:T(8,128)S(1)}, f32[128,256]{1,0:T(8,128)S(1)}, u32[]{:S(2)}, u32[]{:S(2)}) collective-permute-start(f32[128,256]{1,0:T(8,128)S(1)} %right.5.refs_7_), channel_id=1, source_target_pairs={{0,4},{1,5},{2,6},{3,7},{4,0},{5,1},{6,2},{7,3},{8,12},{9,13},{10,... | collective-permute-start | bytes 393224 | tf_op jit(solution)/shard_map/ppermute | solution.py:300
  62.6 7.8 %collective-permute-start.22 = (f32[128,256]{1,0:T(8,128)S(1)}, f32[128,256]{1,0:T(8,128)S(1)}, u32[]{:S(2)}, u32[]{:S(2)}) collective-permute-start(f32[128,256]{1,0:T(8,128)S(1)} %right.5.refs_7_), channel_id=1, source_target_pairs={{0,1},{1,0},{2,3},{3,2},{4,5},{5,4},{6,7},{7,6},{8,9},{9,8},{10,11... | collective-permute-start | bytes 393224 | tf_op jit(solution)/shard_map/ppermute | solution.py:300
  62.8 7.6 %collective-permute-start.34 = (f32[128,256]{1,0:T(8,128)S(1)}, f32[128,256]{1,0:T(8,128)S(1)}, u32[]{:S(2)}, u32[]{:S(2)}) collective-permute-start(f32[128,256]{1,0:T(8,128)S(1)} %right.5.refs_7_), channel_id=1, source_target_pairs={{0,8},{1,9},{2,10},{3,11},{4,12},{5,13},{6,14},{7,15},{8,0},{9,1},... | collective-permute-start | bytes 393224 | tf_op jit(solution)/shard_map/ppermute | solution.py:300
  66.0 7.8 %collective-permute-start.26 = (f32[192,256]{1,0:T(8,128)S(1)}, f32[192,256]{1,0:T(8,128)S(1)}, u32[]{:S(2)}, u32[]{:S(2)}) collective-permute-start(f32[192,256]{1,0:T(8,128)S(1)} %collective-permute-done.25.refs_7_), channel_id=1, source_target_pairs={{0,2},{1,3},{2,0},{3,1},{4,6},{5,7},{6,4},{7,5},{8,10},{9,11},{10,... | collective-permute-start | bytes 589832 | tf_op jit(solution)/shard_map/ppermute | solution.py:300
  67.5 6.7 %collective-permute-start.24 = (f32[192,256]{1,0:T(8,128)S(1)}, f32[192,256]{1,0:T(8,128)S(1)}, u32[]{:S(2)}, u32[]{:S(2)}) collective-permute-start(f32[192,256]{1,0:T(8,128)S(1)} %collective-permute-done.23.refs_5_), channel_id=1, source_target_pairs={{0,4},{1,5},{2,6},{3,7},{4,0},{5,1},{6,2},{7,3},{8,12},{9,13},{10,... | collective-permute-start | bytes 589832 | tf_op jit(solution)/shard_map/ppermute | solution.py:300
  68.5 5.8 %collective-permute-start.28 = (f32[128,256]{1,0:T(8,128)S(1)}, f32[128,256]{1,0:T(8,128)S(1)}, u32[]{:S(2)}, u32[]{:S(2)}) collective-permute-start(f32[128,256]{1,0:T(8,128)S(1)} %collective-permute-done.27.refs_9_), channel_id=1, source_target_pairs={{0,8},{1,9},{2,10},{3,11},{4,12},{5,13},{6,14},{7,15},{8,0},{9,1},... | collective-permute-start | bytes 393224 | tf_op jit(solution)/shard_map/ppermute | solution.py:300
  70.4 4.2 %collective-permute-start.39 = (f32[128,256]{1,0:T(8,128)S(1)}, f32[128,256]{1,0:T(8,128)S(1)}, u32[]{:S(2)}, u32[]{:S(2)}) collective-permute-start(f32[128,256]{1,0:T(8,128)S(1)} %collective-permute-done.27.refs_9_), channel_id=1, source_target_pairs={{0,1},{1,0},{2,3},{3,2},{4,5},{5,4},{6,7},{7,6},{8,9},{9,8},{10,11... | collective-permute-start | bytes 393224 | tf_op jit(solution)/shard_map/ppermute | solution.py:300
  70.4 4.2 %collective-permute-start.40 = (f32[128,256]{1,0:T(8,128)S(1)}, f32[128,256]{1,0:T(8,128)S(1)}, u32[]{:S(2)}, u32[]{:S(2)}) collective-permute-start(f32[128,256]{1,0:T(8,128)S(1)} %collective-permute-done.34.refs_10_), channel_id=1, source_target_pairs={{0,1},{1,0},{2,3},{3,2},{4,5},{5,4},{6,7},{7,6},{8,9},{9,8},{10,11... | collective-permute-start | bytes 393224 | tf_op jit(solution)/shard_map/ppermute | solution.py:300
  73.8 5.2 %collective-permute-start.30 = (f32[192,256]{1,0:T(8,128)S(1)}, f32[192,256]{1,0:T(8,128)S(1)}, u32[]{:S(2)}, u32[]{:S(2)}) collective-permute-start(f32[192,256]{1,0:T(8,128)S(1)} %collective-permute-done.26.refs_6_), channel_id=1, source_target_pairs={{0,1},{1,0},{2,3},{3,2},{4,5},{5,4},{6,7},{7,6},{8,9},{9,8},{10,11... | collective-permute-start | bytes 589832 | tf_op jit(solution)/shard_map/ppermute | solution.py:300
  74.2 4.8 %collective-permute-start.29 = (f32[192,256]{1,0:T(8,128)S(1)}, f32[192,256]{1,0:T(8,128)S(1)}, u32[]{:S(2)}, u32[]{:S(2)}) collective-permute-start(f32[192,256]{1,0:T(8,128)S(1)} %collective-permute-done.24.refs_5_), channel_id=1, source_target_pairs={{0,1},{1,0},{2,3},{3,2},{4,5},{5,4},{6,7},{7,6},{8,9},{9,8},{10,11... | collective-permute-start | bytes 589832 | tf_op jit(solution)/shard_map/ppermute | solution.py:300
  74.3 4.7 %collective-permute-start.31 = (f32[128,256]{1,0:T(8,128)S(1)}, f32[128,256]{1,0:T(8,128)S(1)}, u32[]{:S(2)}, u32[]{:S(2)}) collective-permute-start(f32[128,256]{1,0:T(8,128)S(1)} %collective-permute-done.28.refs_7_), channel_id=1, source_target_pairs={{0,1},{1,0},{2,3},{3,2},{4,5},{5,4},{6,7},{7,6},{8,9},{9,8},{10,11... | collective-permute-start | bytes 393224 | tf_op jit(solution)/shard_map/ppermute | solution.py:300
where the time goes:
time: 83.4 us; the launch traced here: 83.1 us
  starting transfers between devices  43.5 us (52%)
  Pallas kernels  22.1 us (26%)
  waiting for transfers between devices  16.4 us (20%)
  between operations  0.87 us (1%)
    ppermute x41, starting transfers between devices, swap(): return lax.ppermute(x, AXES, [(i, i ^ 1 << bit) for i in range(count)])  43.5 us
    ppermute x41, waiting for transfers between devices, swap(): return lax.ppermute(x, AXES, [(i, i ^ 1 << bit) for i in range(count)])  16.4 us
    pallas_call x3, Pallas kernels, apply_cores(): pl.pallas_call(functools.partial(apply_kernel, shapes, half, first, last)...  11.3 us
    pallas_call x5, Pallas kernels, build(): pl.pallas_call(functools.partial(core_kernel, items, mine, half), out_sha...  4.4 us
    pallas_call x1, Pallas kernels, open_build(): pl.pallas_call(functools.partial(open_kernel, items, half), out_shape=[ja...  3.38 us
  transfers between devices with their start and end apart: 41, of which 9 were waited for; matrix products, arithmetic and copies ran while one was open for 0% of the time, Pallas kernels for 17%

commit v1 on v0

--- a/solution.py
+++ b/solution.py
@@ -12,9 +12,15 @@
 SMEM = pl.BlockSpec(memory_space=pltpu.SMEM)
 TILE = 256
 LOADS = 4
-STAGES = ((0,), (1, 2), (3,))
-
-GROUPS = ((3, (2, 1, 3, 4), "h"), (3, (1, 3, 2, 4), "h"), (2, (3, 2, 4, 1), "d"))
+
+GROUPS = ((3, (2, 1, 3, 4), 'h', 'p'), (3, (1, 3, 2, 4), 'h', 'p'), (2, (3, 2, 1, 4), 'h', 'p'))
+N = len(GROUPS)
+BOTH = (True, False)
+STAGES = (
+    tuple((g, j, m) for g in range(N) for j in (0, 1, 2) for m in BOTH),
+    tuple((g, 3, True) for g in range(N)),
+    tuple((g, 3, False) for g in range(N)),
+)
 
 NT = (((1,), (1,)), ((), ()))
 
@@ -275,10 +281,8 @@
     aliases = {}
     if first:
         outs.append(jax.ShapeDtypeStruct((rank, n), jnp.float32))
-    else:
-        aliases = {len(ops) - 1: 1}
-        if not last:
-            aliases[len(ops) - 2] = 0
+    elif not last:
+        aliases = {len(ops) - 2: 0, len(ops) - 1: 1}
     return pl.pallas_call(
         functools.partial(apply_kernel, shapes, half, first, last),
         out_shape=outs,
@@ -296,23 +300,24 @@
     half = directions.shape[0] // 2
     extra = tuple(range(5, count.bit_length() - 1))
 
-    def swap(x, bit):
-        return lax.ppermute(x, AXES, [(i, i ^ (1 << bit)) for i in range(count)])
+    def swap(x, *bits):
+        mask = sum(1 << bit for bit in bits)
+        return lax.ppermute(x, AXES, [(i, i ^ mask) for i in range(count)])
 
     me = (lax.axis_index("rows") * lax.axis_size("cores") + lax.axis_index("cores")).astype(jnp.int32).reshape(1)
     items = [(j % 2, j // 2) for j in range(2 * half)]
     groups = []
     at = 0
-    for i, (size, bits, mode) in enumerate(GROUPS):
+    for i, (size, bits, mode, back) in enumerate(GROUPS):
         size = len(items) - at if i == len(GROUPS) - 1 else size
-        groups.append((tuple(items[at:at + size]), bits, mode))
+        groups.append((tuple(items[at:at + size]), bits, mode, back))
         at += size
 
     other, f1, f2t, dirs, res = open_build(groups[0][0], half, me, factor_one, factor_two, directions, residual)
     args = (me, f1, f2t, dirs, res)
     others = [swap(other, 0)]
     q, after = [], None
-    for g, (its, bits, mode) in enumerate(groups):
+    for g, (its, bits, mode, _) in enumerate(groups):
         own = build(its, True, half, after, *args)
         if g + 1 < len(groups):
             other = build(groups[g + 1][0], False, half, own, *args)
@@ -320,13 +325,13 @@
         q.append(left(its, bits, mode, me, own, others[g], middle_one))
         after = q[-1][3]
     t = [{} for _ in groups]
-    for (_, bits, mode), v, x in zip(groups, t, q):
+    for (_, bits, mode, _), v, x in zip(groups, t, q):
         v["r11"] = swap(x[3], bits[0])
-    for (_, bits, mode), v, x in zip(groups, t, q):
+    for (_, bits, mode, _), v, x in zip(groups, t, q):
         v["r10"] = swap(x[2], bits[0])
-    for (_, bits, mode), v, x in zip(groups, t, q):
+    for (_, bits, mode, _), v, x in zip(groups, t, q):
         v["r01"] = swap(x[1] + v["r11"], bits[1])
-    for (_, bits, mode), v, x in zip(groups, t, q):
+    for (_, bits, mode, _), v, x in zip(groups, t, q):
         a, b, c = x[0], v["r10"], v["r01"]
         if mode == "h":
             h = a.shape[0] // 2
@@ -335,33 +340,38 @@
         else:
             v["s"] = v["k"] = (a + b) + c
         v["r3"] = swap(v["s"], bits[2])
-    for (_, bits, mode), v in zip(groups, t):
+    for (_, bits, mode, back), v in zip(groups, t):
         v["k"] = v["k"] + v["r3"]
         v["r4"] = swap(v["k"], bits[3])
     for bit in extra:
         for v in t:
             v["k"] = v["k"] + v["r4"]
             v["r4"] = swap(v["k"], bit)
-    for (its, bits, mode), v in zip(groups, t):
+    for (its, bits, mode, _), v in zip(groups, t):
         v["k"] = right(its, v["k"], v["r4"], middle_two)
         if mode == "h":
             v["k"] = jnp.concatenate([v["k"], swap(v["k"], bits[2])])
-    for (_, bits, mode), v in zip(groups, t):
+    for (_, bits, mode, back), v in zip(groups, t):
         v["f"] = {0: v["k"]}
         v["f"][1] = swap(v["k"], bits[1])
         v["f"][2] = swap(v["k"], bits[0])
-    for (_, bits, mode), v in zip(groups, t):
-        v["f"][3] = swap(v["f"][1], bits[0])
+    for (_, bits, mode, back), v in zip(groups, t):
+        if back == "p":
+            v["f"][3] = swap(v["f"][1], bits[0])
+        else:
+            v["f"][3] = swap(v["k"], bits[0], bits[1])
         v["o"] = {}
         for i in range(4):
             v["o"][i] = swap(v["f"][i], 0)
     state = None
     for i, stage in enumerate(STAGES):
         parts = []
-        for mine in (True, False):
-            for (its, bits, mode), v in zip(groups, t):
+        for mine in BOTH:
+            for g, ((its, bits, mode, _), v) in enumerate(zip(groups, t)):
                 arrays = v["f" if mine else "o"]
-                parts.append((its, bits, mode, mine, {j: arrays[j] for j in stage}))
+                quarters = {j: arrays[j] for h, j, m in stage if (h, m) == (g, mine)}
+                if quarters:
+                    parts.append((its, bits, mode, mine, quarters))
         state = apply_cores(
             parts, half, me, f1, f2t, dirs, res, state, i == len(STAGES) - 1
         )

time: 83.4 us -> 87.2 us (1.046)
  waiting for transfers between devices: 16.4 us -> 27.1 us
  starting transfers between devices: 43.5 us -> 39.7 us
  Pallas kernels: 22.1 us -> 19.1 us
    ppermute x41 -> x42, waiting for transfers between devices: 16.4 us -> 27.1 us  [swap(): return lax.ppermute(x, AXES, [(i, i ^ mask) for i in range(count)])]
    ppermute x41 -> x42, starting transfers between devices: 43.5 us -> 39.7 us  [swap(): return lax.ppermute(x, AXES, [(i, i ^ mask) for i in range(count)])]
    pallas_call x3, Pallas kernels: 11.3 us -> 8.33 us  [apply_cores(): pl.pallas_call(functools.partial(apply_kernel, shapes, half, first, last)...]
  transfers between devices with their start and end apart: 41 -> 42, of which waited for: 9 -> 12; matrix products, arithmetic and copies ran while one was open for 0% -> 0% of each run, Pallas kernels for 17% -> 15%
where the time goes in v1:
time: 87.2 us; the launch traced here: 87.1 us
  starting transfers between devices  39.7 us (46%)
  waiting for transfers between devices  27.1 us (31%)
  Pallas kernels  19.1 us (22%)
  between operations  0.9 us (1%)
    ppermute x42, starting transfers between devices, swap(): return lax.ppermute(x, AXES, [(i, i ^ mask) for i in range(count)])  39.7 us
    ppermute x42, waiting for transfers between devices, swap(): return lax.ppermute(x, AXES, [(i, i ^ mask) for i in range(count)])  27.1 us
    pallas_call x3, Pallas kernels, apply_cores(): pl.pallas_call(functools.partial(apply_kernel, shapes, half, first, last)...  8.33 us
    pallas_call x5, Pallas kernels, build(): pl.pallas_call(functools.partial(core_kernel, items, mine, half), out_sha...  4.4 us
    pallas_call x1, Pallas kernels, open_build(): pl.pallas_call(functools.partial(open_kernel, items, half), out_shape=[ja...  3.38 us
  transfers between devices with their start and end apart: 42, of which 12 were waited for; matrix products, arithmetic and copies ran while one was open for 0% of the time, Pallas kernels for 15%

profile of v1, /device:TPU:0, one launch (start us, length us, event | category | flops | bytes accessed | tf_op | source)
XLA Modules:
  0.0 87.1 jit_solution(2081664927719699496)
XLA Ops:
  0.6 3.4 %cores_open.1 = (f32[768,256]{1,0:T(8,128)S(1)}, bf16[2048,256]{1,0:T(8,128)(2,1)S(1)}, bf16[256,2048]{1,0:T(8,128)(2,1)S(1)}, f32[8,2048]{1,0:T(8,128)S(1)}, f32[8,2048]{1,0:T(8,128)S(1)}) custom-call(s32[1]{0:T(128)} %bitcast.s_ref.refs_0_, bf16[2048,256]{1,0:T(8,128)(2,1)} %f1_in.1, bf16[2048,256]{1,0:T(8,128)(2,1)} %f2_in.1, f32[8,2048]{1,0:T(8,128)} %dirs_in.1, ...), custom_call_target="tpu_custom_call" | custom-call | flops 805306368 | bytes 2097152 | tf_op jit(solution)/shard_map/cores_open/pallas_call | solution.py:105
  4.0 0.6 collective-permute-start
  4.6 1.0 %shard_map.77.a_ref.refs_0_ = f32[768,256]{1,0:T(8,128)S(1)} custom-call(s32[1]{0:T(128)} %bitcast.s_ref.refs_0_, bf16[2048,256]{1,0:T(8,128)(2,1)S(1)} %get-tuple-element.26.f1_ref.refs_1_, bf16[256,2048]{1,0:T(8,128)(2,1)S(1)} %get-tuple-element.27.f2t_ref.refs_2_, f32[8,2048]{1,0:T(8,128)S(1)} %get-tuple-element.28.dirs_ref.refs_3_, ...), custom_call_target="tpu_custom_call" | custom-call | flops 805306368 | bytes 2097152 | tf_op jit(solution)/shard_map/pallas_call | solution.py:141
  5.6 1.0 %shard_map.79 = f32[768,256]{1,0:T(8,128)S(1)} custom-call(s32[1]{0:T(128)} %bitcast.s_ref.refs_0_, bf16[2048,256]{1,0:T(8,128)(2,1)S(1)} %get-tuple-element.26.f1_ref.refs_1_, bf16[256,2048]{1,0:T(8,128)(2,1)S(1)} %get-tuple-element.27.f2t_ref.refs_2_, f32[8,2048]{1,0:T(8,128)S(1)} %get-tuple-element.28.dirs_ref.refs_3_, ...), custom_call_target="tpu_custom_call" | custom-call | flops 805306368 | bytes 2097152 | tf_op jit(solution)/shard_map/pallas_call | solution.py:141
  6.7 0.6 left.3
  7.3 1.0 %shard_map.78.a_ref.refs_0_ = f32[768,256]{1,0:T(8,128)S(1)} custom-call(s32[1]{0:T(128)} %bitcast.s_ref.refs_0_, bf16[2048,256]{1,0:T(8,128)(2,1)S(1)} %get-tuple-element.26.f1_ref.refs_1_, bf16[256,2048]{1,0:T(8,128)(2,1)S(1)} %get-tuple-element.27.f2t_ref.refs_2_, f32[8,2048]{1,0:T(8,128)S(1)} %get-tuple-element.28.dirs_ref.refs_3_, ...), custom_call_target="tpu_custom_call" | custom-call | flops 805306368 | bytes 2097152 | tf_op jit(solution)/shard_map/pallas_call | solution.py:141
  8.3 0.7 collective-permute-done.9.b_ref
  8.9 0.6 left.4
  9.5 2.7 %collective-permute-start.11 = (f32[192,256]{1,0:T(8,128)S(1)}, f32[192,256]{1,0:T(8,128)S(1)}, u32[]{:S(2)}, u32[]{:S(2)}) collective-permute-start(f32[192,256]{1,0:T(8,128)S(1)} %get-tuple-element.38.refs_0_), channel_id=1, source_target_pairs={{0,2},{1,3},{2,0},{3,1},{4,6},{5,7},{6,4},{7,5},{8,10},{9,11},{10,... | collective-permute-start | bytes 589832 | tf_op jit(solution)/shard_map/ppermute | solution.py:305
  12.2 1.5 %collective-permute-start.2 = (f32[192,256]{1,0:T(8,128)S(1)}, f32[192,256]{1,0:T(8,128)S(1)}, u32[]{:S(2)}, u32[]{:S(2)}) collective-permute-start(f32[192,256]{1,0:T(8,128)S(1)} %get-tuple-element.34.refs_0_), channel_id=1, source_target_pairs={{0,4},{1,5},{2,6},{3,7},{4,0},{5,1},{6,2},{7,3},{8,12},{9,13},{10,... | collective-permute-start | bytes 589832 | tf_op jit(solution)/shard_map/ppermute | solution.py:305
  13.7 0.5 collective-permute-start.10
  14.2 3.8 %collective-permute-done.11 = f32[192,256]{1,0:T(8,128)S(1)} collective-permute-done((f32[192,256]{1,0:T(8,128)S(1)}, f32[192,256]{1,0:T(8,128)S(1)}, u32[]{:S(2)}, u32[]{:S(2)}) %collective-permute-start.11) | collective-permute-done | bytes 196640 | tf_op jit(solution)/shard_map/ppermute | solution.py:305
  18.0 2.1 %collective-permute-start.12 = (f32[192,256]{1,0:T(8,128)S(1)}, f32[192,256]{1,0:T(8,128)S(1)}, u32[]{:S(2)}, u32[]{:S(2)}) collective-permute-start(f32[192,256]{1,0:T(8,128)S(1)} %add.65), channel_id=1, source_target_pairs={{0,8},{1,9},{2,10},{3,11},{4,12},{5,13},{6,14},{7,15},{8,0},{9,1},... | collective-permute-start | bytes 589832 | tf_op jit(solution)/shard_map/ppermute | solution.py:305
  20.2 0.7 shard_map.81
  21.0 1.6 %collective-permute-start.1 = (f32[192,256]{1,0:T(8,128)S(1)}, f32[192,256]{1,0:T(8,128)S(1)}, u32[]{:S(2)}, u32[]{:S(2)}) collective-permute-start(f32[192,256]{1,0:T(8,128)S(1)} %get-tuple-element.32), channel_id=1, source_target_pairs={{0,4},{1,5},{2,6},{3,7},{4,0},{5,1},{6,2},{7,3},{8,12},{9,13},{10,... | collective-permute-start | bytes 589832 | tf_op jit(solution)/shard_map/ppermute | solution.py:305
  22.5 0.7 shard_map.80.a_ref
  23.3 1.6 %collective-permute-start.3 = (f32[192,256]{1,0:T(8,128)S(1)}, f32[192,256]{1,0:T(8,128)S(1)}, u32[]{:S(2)}, u32[]{:S(2)}) collective-permute-start(f32[192,256]{1,0:T(8,128)S(1)} %add.59), channel_id=1, source_target_pairs={{0,2},{1,3},{2,0},{3,1},{4,6},{5,7},{6,4},{7,5},{8,10},{9,11},{10,... | collective-permute-start | bytes 589832 | tf_op jit(solution)/shard_map/ppermute | solution.py:305
  24.9 1.0 %collective-permute-start.13 = (f32[96,256]{1,0:T(8,128)S(1)}, f32[96,256]{1,0:T(8,128)S(1)}, u32[]{:S(2)}, u32[]{:S(2)}) collective-permute-start(f32[96,256]{1,0:T(8,128)S(1)} %slice_add_fusion), channel_id=1, source_target_pairs={{0,4},{1,5},{2,6},{3,7},{4,0},{5,1},{6,2},{7,3},{8,12},{9,13},{10,... | collective-permute-start | bytes 294920 | tf_op jit(solution)/shard_map/ppermute | solution.py:305
  25.9 2.9 %collective-permute-done.1 = f32[192,256]{1,0:T(8,128)S(1)} collective-permute-done((f32[192,256]{1,0:T(8,128)S(1)}, f32[192,256]{1,0:T(8,128)S(1)}, u32[]{:S(2)}, u32[]{:S(2)}) %collective-permute-start.1) | collective-permute-done | bytes 196640 | tf_op jit(solution)/shard_map/ppermute | solution.py:305
  28.8 1.5 %collective-permute-done.3 = f32[192,256]{1,0:T(8,128)S(1)} collective-permute-done((f32[192,256]{1,0:T(8,128)S(1)}, f32[192,256]{1,0:T(8,128)S(1)}, u32[]{:S(2)}, u32[]{:S(2)}) %collective-permute-start.3) | collective-permute-done | bytes 196640 | tf_op jit(solution)/shard_map/ppermute | solution.py:305
  30.4 0.5 collective-permute-start.4
  30.9 2.7 %collective-permute-start.14 = (f32[96,256]{1,0:T(8,128)S(1)}, f32[96,256]{1,0:T(8,128)S(1)}, u32[]{:S(2)}, u32[]{:S(2)}) collective-permute-start(f32[96,256]{1,0:T(8,128)S(1)} %fusion.a_ref), channel_id=1, source_target_pairs={{0,16},{1,17},{2,18},{3,19},{4,20},{5,21},{6,22},{7,23},{8,24},{9,... | collective-permute-start | bytes 294920 | tf_op jit(solution)/shard_map/ppermute | solution.py:305
  34.0 1.6 %collective-permute-start.20 = (f32[128,256]{1,0:T(8,128)S(1)}, f32[128,256]{1,0:T(8,128)S(1)}, u32[]{:S(2)}, u32[]{:S(2)}) collective-permute-start(f32[128,256]{1,0:T(8,128)S(1)} %get-tuple-element.42), channel_id=1, source_target_pairs={{0,8},{1,9},{2,10},{3,11},{4,12},{5,13},{6,14},{7,15},{8,0},{9,1},... | collective-permute-start | bytes 393224 | tf_op jit(solution)/shard_map/ppermute | solution.py:305
  35.9 2.9 %collective-permute-start.5 = (f32[96,256]{1,0:T(8,128)S(1)}, f32[96,256]{1,0:T(8,128)S(1)}, u32[]{:S(2)}, u32[]{:S(2)}) collective-permute-start(f32[96,256]{1,0:T(8,128)S(1)} %fusion.1.a_ref), channel_id=1, source_target_pairs={{0,16},{1,17},{2,18},{3,19},{4,20},{5,21},{6,22},{7,23},{8,24},{9,... | collective-permute-start | bytes 294920 | tf_op jit(solution)/shard_map/ppermute | solution.py:305
  38.8 0.5 right.4
  39.3 0.6 collective-permute-start.15
  39.9 2.0 %collective-permute-start.19 = (f32[128,256]{1,0:T(8,128)S(1)}, f32[128,256]{1,0:T(8,128)S(1)}, u32[]{:S(2)}, u32[]{:S(2)}) collective-permute-start(f32[128,256]{1,0:T(8,128)S(1)} %get-tuple-element.40), channel_id=1, source_target_pairs={{0,8},{1,9},{2,10},{3,11},{4,12},{5,13},{6,14},{7,15},{8,0},{9,1},... | collective-permute-start | bytes 393224 | tf_op jit(solution)/shard_map/ppermute | solution.py:305
  41.9 1.6 %collective-permute-start.21 = (f32[128,256]{1,0:T(8,128)S(1)}, f32[128,256]{1,0:T(8,128)S(1)}, u32[]{:S(2)}, u32[]{:S(2)}) collective-permute-start(f32[128,256]{1,0:T(8,128)S(1)} %add.71), channel_id=1, source_target_pairs={{0,4},{1,5},{2,6},{3,7},{4,0},{5,1},{6,2},{7,3},{8,12},{9,13},{10,... | collective-permute-start | bytes 393224 | tf_op jit(solution)/shard_map/ppermute | solution.py:305
  43.5 0.5 right.3
  43.9 2.0 %collective-permute-start.6 = (f32[96,256]{1,0:T(8,128)S(1)}, f32[96,256]{1,0:T(8,128)S(1)}, u32[]{:S(2)}, u32[]{:S(2)}) collective-permute-start(f32[96,256]{1,0:T(8,128)S(1)} %right.3), channel_id=1, source_target_pairs={{0,8},{1,9},{2,10},{3,11},{4,12},{5,13},{6,14},{7,15},{8,0},{9,1},... | collective-permute-start | bytes 294920 | tf_op jit(solution)/shard_map/ppermute | solution.py:305
  46.1 1.5 %collective-permute-start.17 = (f32[192,256]{1,0:T(8,128)S(1)}, f32[192,256]{1,0:T(8,128)S(1)}, u32[]{:S(2)}, u32[]{:S(2)}) collective-permute-start(f32[192,256]{1,0:T(8,128)S(1)} %pad_maximum_fusion.1.refs_8_), channel_id=1, source_target_pairs={{0,2},{1,3},{2,0},{3,1},{4,6},{5,7},{6,4},{7,5},{8,10},{9,11},{10,... | collective-permute-start | bytes 589832 | tf_op jit(solution)/shard_map/ppermute | solution.py:305
  47.6 0.9 %collective-permute-start.22 = (f32[64,256]{1,0:T(8,128)S(1)}, f32[64,256]{1,0:T(8,128)S(1)}, u32[]{:S(2)}, u32[]{:S(2)}) collective-permute-start(f32[64,256]{1,0:T(8,128)S(1)} %slice_add_fusion.8), channel_id=1, source_target_pairs={{0,2},{1,3},{2,0},{3,1},{4,6},{5,7},{6,4},{7,5},{8,10},{9,11},{10,... | collective-permute-start | bytes 196616 | tf_op jit(solution)/shard_map/ppermute | solution.py:305
  48.5 0.6 collective-permute-done.6
  49.1 1.6 %collective-permute-start.7 = (f32[192,256]{1,0:T(8,128)S(1)}, f32[192,256]{1,0:T(8,128)S(1)}, u32[]{:S(2)}, u32[]{:S(2)}) collective-permute-start(f32[192,256]{1,0:T(8,128)S(1)} %pad_maximum_fusion.refs_5_), channel_id=1, source_target_pairs={{0,2},{1,3},{2,0},{3,1},{4,6},{5,7},{6,4},{7,5},{8,10},{9,11},{10,... | collective-permute-start | bytes 589832 | tf_op jit(solution)/shard_map/ppermute | solution.py:305
  50.7 3.4 %collective-permute-done.22 = f32[64,256]{1,0:T(8,128)S(1)} collective-permute-done((f32[64,256]{1,0:T(8,128)S(1)}, f32[64,256]{1,0:T(8,128)S(1)}, u32[]{:S(2)}, u32[]{:S(2)}) %collective-permute-start.22) | collective-permute-done | bytes 65568 | tf_op jit(solution)/shard_map/ppermute | solution.py:305
  54.7 2.8 %collective-permute-start.23 = (f32[64,256]{1,0:T(8,128)S(1)}, f32[64,256]{1,0:T(8,128)S(1)}, u32[]{:S(2)}, u32[]{:S(2)}) collective-permute-start(f32[64,256]{1,0:T(8,128)S(1)} %fusion.2.a_ref), channel_id=1, source_target_pairs={{0,16},{1,17},{2,18},{3,19},{4,20},{5,21},{6,22},{7,23},{8,24},{9,... | collective-permute-start | bytes 196616 | tf_op jit(solution)/shard_map/ppermute | solution.py:305
  57.7 3.9 %collective-permute-done.23.b_ref = f32[64,256]{1,0:T(8,128)S(1)} collective-permute-done((f32[64,256]{1,0:T(8,128)S(1)}, f32[64,256]{1,0:T(8,128)S(1)}, u32[]{:S(2)}, u32[]{:S(2)}) %collective-permute-start.23) | collective-permute-done | bytes 65568 | tf_op jit(solution)/shard_map/ppermute | solution.py:305
  62.0 2.4 %collective-permute-start.24 = (f32[64,256]{1,0:T(8,128)S(1)}, f32[64,256]{1,0:T(8,128)S(1)}, u32[]{:S(2)}, u32[]{:S(2)}) collective-permute-start(f32[64,256]{1,0:T(8,128)S(1)} %right.5), channel_id=1, source_target_pairs={{0,2},{1,3},{2,0},{3,1},{4,6},{5,7},{6,4},{7,5},{8,10},{9,11},{10,... | collective-permute-start | bytes 196616 | tf_op jit(solution)/shard_map/ppermute | solution.py:305
  65.1 2.2 %collective-permute-done.24 = f32[64,256]{1,0:T(8,128)S(1)} collective-permute-done((f32[64,256]{1,0:T(8,128)S(1)}, f32[64,256]{1,0:T(8,128)S(1)}, u32[]{:S(2)}, u32[]{:S(2)}) %collective-permute-start.24) | collective-permute-done | bytes 65568 | tf_op jit(solution)/shard_map/ppermute | solution.py:305
  67.5 2.0 %collective-permute-start.26 = (f32[128,256]{1,0:T(8,128)S(1)}, f32[128,256]{1,0:T(8,128)S(1)}, u32[]{:S(2)}, u32[]{:S(2)}) collective-permute-start(f32[128,256]{1,0:T(8,128)S(1)} %pad_maximum_fusion.2.refs_11_), channel_id=1, source_target_pairs={{0,8},{1,9},{2,10},{3,11},{4,12},{5,13},{6,14},{7,15},{8,0},{9,1},... | collective-permute-start | bytes 393224 | tf_op jit(solution)/shard_map/ppermute | solution.py:305
  69.6 4.1 %collective-permute-done.25.refs_12_ = f32[128,256]{1,0:T(8,128)S(1)} collective-permute-done((f32[128,256]{1,0:T(8,128)S(1)}, f32[128,256]{1,0:T(8,128)S(1)}, u32[]{:S(2)}, u32[]{:S(2)}) %collective-permute-start.25) | collective-permute-done | bytes 131104 | tf_op jit(solution)/shard_map/ppermute | solution.py:305
  73.9 0.5 collective-permute-start.35
  74.4 3.0 %collective-permute-done.36.refs_5_ = f32[192,256]{1,0:T(8,128)S(1)} collective-permute-done((f32[192,256]{1,0:T(8,128)S(1)}, f32[192,256]{1,0:T(8,128)S(1)}, u32[]{:S(2)}, u32[]{:S(2)}) %collective-permute-start.36) | collective-permute-done | bytes 196640 | tf_op jit(solution)/shard_map/ppermute | solution.py:305
  77.4 0.5 collective-permute-start.37
  78.0 0.7 collective-permute-done.40.refs_7_
  78.7 5.0 %apply.2 = (f32[256,2048]{1,0:T(8,128)S(1)}, f32[8,2048]{1,0:T(8,128)S(1)}, f32[256,2048]{1,0:T(8,128)S(1)}) custom-call(s32[1]{0:T(128)} %bitcast.s_ref.refs_0_, bf16[2048,256]{1,0:T(8,128)(2,1)S(1)} %get-tuple-element.26.f1_ref.refs_1_, bf16[256,2048]{1,0:T(8,128)(2,1)S(1)} %get-tuple-element.27.f2t_ref.refs_2_, ...), custom_call_target="tpu_custom_call" | custom-call | flops 3221225472 | bytes 4194304 | tf_op jit(solution)/shard_map/apply/pallas_call | solution.py:286
  83.7 0.8 apply.3
  84.5 2.5 %apply_last.1 = (f32[2048,256]{1,0:T(8,128)}, f32[8,2048]{1,0:T(8,128)}) custom-call(s32[1]{0:T(128)} %bitcast.s_ref.refs_0_, f32[256,2048]{1,0:T(8,128)S(1)} %get-tuple-element.43.refs_1_, bf16[256,2048]{1,0:T(8,128)(2,1)S(1)} %get-tuple-element.27.f2t_ref.refs_2_, f32[8,2048]{1,0:T(8,128)S(1)} %get-tuple-element.28.dirs_ref.refs_3_, ...), custom_call_target="tpu_custom_call" | custom-call | flops 536870912 | bytes 4194304 | tf_op jit(solution)/shard_map/apply_last/pallas_call | solution.py:286
  (67 shorter events, 3.4 us)
Async XLA Ops:
  4.0 2.6 %collective-permute-start = (f32[768,256]{1,0:T(8,128)S(1)}, f32[768,256]{1,0:T(8,128)S(1)}, u32[]{:S(2)}, u32[]{:S(2)}) collective-permute-start(f32[768,256]{1,0:T(8,128)S(1)} %get-tuple-element.30), channel_id=1, source_target_pairs={{0,1},{1,0},{2,3},{3,2},{4,5},{5,4},{6,7},{7,6},{8,9},{9,8},{10,11... | collective-permute-start | bytes 2359304 | tf_op jit(solution)/shard_map/ppermute | solution.py:305
  5.6 1.1 %copy-start.1 = (f32[256,256]{1,0:T(8,128)S(1)}, f32[256,256]{1,0:T(8,128)}, u32[]{:S(2)}) copy-start(f32[256,256]{1,0:T(8,128)} %m1_ref.5) | copy-start | bytes 786436
  6.6 2.4 %collective-permute-start.9 = (f32[768,256]{1,0:T(8,128)S(1)}, f32[768,256]{1,0:T(8,128)S(1)}, u32[]{:S(2)}, u32[]{:S(2)}) collective-permute-start(f32[768,256]{1,0:T(8,128)S(1)} %shard_map.79), channel_id=1, source_target_pairs={{0,1},{1,0},{2,3},{3,2},{4,5},{5,4},{6,7},{7,6},{8,9},{9,8},{10,11... | collective-permute-start | bytes 2359304 | tf_op jit(solution)/shard_map/ppermute | solution.py:305
  9.5 8.5 %collective-permute-start.11 = (f32[192,256]{1,0:T(8,128)S(1)}, f32[192,256]{1,0:T(8,128)S(1)}, u32[]{:S(2)}, u32[]{:S(2)}) collective-permute-start(f32[192,256]{1,0:T(8,128)S(1)} %get-tuple-element.38.refs_0_), channel_id=1, source_target_pairs={{0,2},{1,3},{2,0},{3,1},{4,6},{5,7},{6,4},{7,5},{8,10},{9,11},{10,... | collective-permute-start | bytes 589832 | tf_op jit(solution)/shard_map/ppermute | solution.py:305
  12.2 11.0 %collective-permute-start.2 = (f32[192,256]{1,0:T(8,128)S(1)}, f32[192,256]{1,0:T(8,128)S(1)}, u32[]{:S(2)}, u32[]{:S(2)}) collective-permute-start(f32[192,256]{1,0:T(8,128)S(1)} %get-tuple-element.34.refs_0_), channel_id=1, source_target_pairs={{0,4},{1,5},{2,6},{3,7},{4,0},{5,1},{6,2},{7,3},{8,12},{9,13},{10,... | collective-permute-start | bytes 589832 | tf_op jit(solution)/shard_map/ppermute | solution.py:305
  13.7 11.2 %collective-permute-start.10 = (f32[192,256]{1,0:T(8,128)S(1)}, f32[192,256]{1,0:T(8,128)S(1)}, u32[]{:S(2)}, u32[]{:S(2)}) collective-permute-start(f32[192,256]{1,0:T(8,128)S(1)} %get-tuple-element.36), channel_id=1, source_target_pairs={{0,2},{1,3},{2,0},{3,1},{4,6},{5,7},{6,4},{7,5},{8,10},{9,11},{10,... | collective-permute-start | bytes 589832 | tf_op jit(solution)/shard_map/ppermute | solution.py:305
  18.0 6.9 %collective-permute-start.12 = (f32[192,256]{1,0:T(8,128)S(1)}, f32[192,256]{1,0:T(8,128)S(1)}, u32[]{:S(2)}, u32[]{:S(2)}) collective-permute-start(f32[192,256]{1,0:T(8,128)S(1)} %add.65), channel_id=1, source_target_pairs={{0,8},{1,9},{2,10},{3,11},{4,12},{5,13},{6,14},{7,15},{8,0},{9,1},... | collective-permute-start | bytes 589832 | tf_op jit(solution)/shard_map/ppermute | solution.py:305
  20.9 12.7 %collective-permute-start.18 = (f32[512,256]{1,0:T(8,128)S(1)}, f32[512,256]{1,0:T(8,128)S(1)}, u32[]{:S(2)}, u32[]{:S(2)}) collective-permute-start(f32[512,256]{1,0:T(8,128)S(1)} %shard_map.81), channel_id=1, source_target_pairs={{0,1},{1,0},{2,3},{3,2},{4,5},{5,4},{6,7},{7,6},{8,9},{9,8},{10,11... | collective-permute-start | bytes 1572872 | tf_op jit(solution)/shard_map/ppermute | solution.py:305
  21.0 7.8 %collective-permute-start.1 = (f32[192,256]{1,0:T(8,128)S(1)}, f32[192,256]{1,0:T(8,128)S(1)}, u32[]{:S(2)}, u32[]{:S(2)}) collective-permute-start(f32[192,256]{1,0:T(8,128)S(1)} %get-tuple-element.32), channel_id=1, source_target_pairs={{0,4},{1,5},{2,6},{3,7},{4,0},{5,1},{6,2},{7,3},{8,12},{9,13},{10,... | collective-permute-start | bytes 589832 | tf_op jit(solution)/shard_map/ppermute | solution.py:305
  23.2 15.5 %copy-start = (f32[256,256]{1,0:T(8,128)S(1)}, f32[256,256]{1,0:T(8,128)}, u32[]{:S(2)}) copy-start(f32[256,256]{1,0:T(8,128)} %m2_ref.5) | copy-start | bytes 786436
  23.3 7.0 %collective-permute-start.3 = (f32[192,256]{1,0:T(8,128)S(1)}, f32[192,256]{1,0:T(8,128)S(1)}, u32[]{:S(2)}, u32[]{:S(2)}) collective-permute-start(f32[192,256]{1,0:T(8,128)S(1)} %add.59), channel_id=1, source_target_pairs={{0,2},{1,3},{2,0},{3,1},{4,6},{5,7},{6,4},{7,5},{8,10},{9,11},{10,... | collective-permute-start | bytes 589832 | tf_op jit(solution)/shard_map/ppermute | solution.py:305
  24.9 6.0 %collective-permute-start.13 = (f32[96,256]{1,0:T(8,128)S(1)}, f32[96,256]{1,0:T(8,128)S(1)}, u32[]{:S(2)}, u32[]{:S(2)}) collective-permute-start(f32[96,256]{1,0:T(8,128)S(1)} %slice_add_fusion), channel_id=1, source_target_pairs={{0,4},{1,5},{2,6},{3,7},{4,0},{5,1},{6,2},{7,3},{8,12},{9,13},{10,... | collective-permute-start | bytes 294920 | tf_op jit(solution)/shard_map/ppermute | solution.py:305
  30.4 5.5 %collective-permute-start.4 = (f32[96,256]{1,0:T(8,128)S(1)}, f32[96,256]{1,0:T(8,128)S(1)}, u32[]{:S(2)}, u32[]{:S(2)}) collective-permute-start(f32[96,256]{1,0:T(8,128)S(1)} %slice_add_fusion.4), channel_id=1, source_target_pairs={{0,8},{1,9},{2,10},{3,11},{4,12},{5,13},{6,14},{7,15},{8,0},{9,1},... | collective-permute-start | bytes 294920 | tf_op jit(solution)/shard_map/ppermute | solution.py:305
  30.9 7.9 %collective-permute-start.14 = (f32[96,256]{1,0:T(8,128)S(1)}, f32[96,256]{1,0:T(8,128)S(1)}, u32[]{:S(2)}, u32[]{:S(2)}) collective-permute-start(f32[96,256]{1,0:T(8,128)S(1)} %fusion.a_ref), channel_id=1, source_target_pairs={{0,16},{1,17},{2,18},{3,19},{4,20},{5,21},{6,22},{7,23},{8,24},{9,... | collective-permute-start | bytes 294920 | tf_op jit(solution)/shard_map/ppermute | solution.py:305
  34.0 7.9 %collective-permute-start.20 = (f32[128,256]{1,0:T(8,128)S(1)}, f32[128,256]{1,0:T(8,128)S(1)}, u32[]{:S(2)}, u32[]{:S(2)}) collective-permute-start(f32[128,256]{1,0:T(8,128)S(1)} %get-tuple-element.42), channel_id=1, source_target_pairs={{0,8},{1,9},{2,10},{3,11},{4,12},{5,13},{6,14},{7,15},{8,0},{9,1},... | collective-permute-start | bytes 393224 | tf_op jit(solution)/shard_map/ppermute | solution.py:305
  35.9 7.6 %collective-permute-start.5 = (f32[96,256]{1,0:T(8,128)S(1)}, f32[96,256]{1,0:T(8,128)S(1)}, u32[]{:S(2)}, u32[]{:S(2)}) collective-permute-start(f32[96,256]{1,0:T(8,128)S(1)} %fusion.1.a_ref), channel_id=1, source_target_pairs={{0,16},{1,17},{2,18},{3,19},{4,20},{5,21},{6,22},{7,23},{8,24},{9,... | collective-permute-start | bytes 294920 | tf_op jit(solution)/shard_map/ppermute | solution.py:305
  39.3 6.6 %collective-permute-start.15 = (f32[96,256]{1,0:T(8,128)S(1)}, f32[96,256]{1,0:T(8,128)S(1)}, u32[]{:S(2)}, u32[]{:S(2)}) collective-permute-start(f32[96,256]{1,0:T(8,128)S(1)} %right.4), channel_id=1, source_target_pairs={{0,4},{1,5},{2,6},{3,7},{4,0},{5,1},{6,2},{7,3},{8,12},{9,13},{10,... | collective-permute-start | bytes 294920 | tf_op jit(solution)/shard_map/ppermute | solution.py:305
  39.9 7.7 %collective-permute-start.19 = (f32[128,256]{1,0:T(8,128)S(1)}, f32[128,256]{1,0:T(8,128)S(1)}, u32[]{:S(2)}, u32[]{:S(2)}) collective-permute-start(f32[128,256]{1,0:T(8,128)S(1)} %get-tuple-element.40), channel_id=1, source_target_pairs={{0,8},{1,9},{2,10},{3,11},{4,12},{5,13},{6,14},{7,15},{8,0},{9,1},... | collective-permute-start | bytes 393224 | tf_op jit(solution)/shard_map/ppermute | solution.py:305
  41.9 5.7 %collective-permute-start.21 = (f32[128,256]{1,0:T(8,128)S(1)}, f32[128,256]{1,0:T(8,128)S(1)}, u32[]{:S(2)}, u32[]{:S(2)}) collective-permute-start(f32[128,256]{1,0:T(8,128)S(1)} %add.71), channel_id=1, source_target_pairs={{0,4},{1,5},{2,6},{3,7},{4,0},{5,1},{6,2},{7,3},{8,12},{9,13},{10,... | collective-permute-start | bytes 393224 | tf_op jit(solution)/shard_map/ppermute | solution.py:305
  43.9 5.2 %collective-permute-start.6 = (f32[96,256]{1,0:T(8,128)S(1)}, f32[96,256]{1,0:T(8,128)S(1)}, u32[]{:S(2)}, u32[]{:S(2)}) collective-permute-start(f32[96,256]{1,0:T(8,128)S(1)} %right.3), channel_id=1, source_target_pairs={{0,8},{1,9},{2,10},{3,11},{4,12},{5,13},{6,14},{7,15},{8,0},{9,1},... | collective-permute-start | bytes 294920 | tf_op jit(solution)/shard_map/ppermute | solution.py:305
  45.9 8.7 %collective-permute-start.16 = (f32[192,256]{1,0:T(8,128)S(1)}, f32[192,256]{1,0:T(8,128)S(1)}, u32[]{:S(2)}, u32[]{:S(2)}) collective-permute-start(f32[192,256]{1,0:T(8,128)S(1)} %pad_maximum_fusion.1.refs_8_), channel_id=1, source_target_pairs={{0,8},{1,9},{2,10},{3,11},{4,12},{5,13},{6,14},{7,15},{8,0},{9,1},... | collective-permute-start | bytes 589832 | tf_op jit(solution)/shard_map/ppermute | solution.py:305
  46.1 8.6 %collective-permute-start.17 = (f32[192,256]{1,0:T(8,128)S(1)}, f32[192,256]{1,0:T(8,128)S(1)}, u32[]{:S(2)}, u32[]{:S(2)}) collective-permute-start(f32[192,256]{1,0:T(8,128)S(1)} %pad_maximum_fusion.1.refs_8_), channel_id=1, source_target_pairs={{0,2},{1,3},{2,0},{3,1},{4,6},{5,7},{6,4},{7,5},{8,10},{9,11},{10,... | collective-permute-start | bytes 589832 | tf_op jit(solution)/shard_map/ppermute | solution.py:305
  47.6 9.9 %collective-permute-start.30 = (f32[192,256]{1,0:T(8,128)S(1)}, f32[192,256]{1,0:T(8,128)S(1)}, u32[]{:S(2)}, u32[]{:S(2)}) collective-permute-start(f32[192,256]{1,0:T(8,128)S(1)} %pad_maximum_fusion.1.refs_8_), channel_id=1, source_target_pairs={{0,1},{1,0},{2,3},{3,2},{4,5},{5,4},{6,7},{7,6},{8,9},{9,8},{10,11... | collective-permute-start | bytes 589832 | tf_op jit(solution)/shard_map/ppermute | solution.py:305
  47.6 6.5 %collective-permute-start.22 = (f32[64,256]{1,0:T(8,128)S(1)}, f32[64,256]{1,0:T(8,128)S(1)}, u32[]{:S(2)}, u32[]{:S(2)}) collective-permute-start(f32[64,256]{1,0:T(8,128)S(1)} %slice_add_fusion.8), channel_id=1, source_target_pairs={{0,2},{1,3},{2,0},{3,1},{4,6},{5,7},{6,4},{7,5},{8,10},{9,11},{10,... | collective-permute-start | bytes 196616 | tf_op jit(solution)/shard_map/ppermute | solution.py:305
  49.1 12.9 %collective-permute-start.7 = (f32[192,256]{1,0:T(8,128)S(1)}, f32[192,256]{1,0:T(8,128)S(1)}, u32[]{:S(2)}, u32[]{:S(2)}) collective-permute-start(f32[192,256]{1,0:T(8,128)S(1)} %pad_maximum_fusion.refs_5_), channel_id=1, source_target_pairs={{0,2},{1,3},{2,0},{3,1},{4,6},{5,7},{6,4},{7,5},{8,10},{9,11},{10,... | collective-permute-start | bytes 589832 | tf_op jit(solution)/shard_map/ppermute | solution.py:305
  54.2 10.3 %collective-permute-start.8 = (f32[192,256]{1,0:T(8,128)S(1)}, f32[192,256]{1,0:T(8,128)S(1)}, u32[]{:S(2)}, u32[]{:S(2)}) collective-permute-start(f32[192,256]{1,0:T(8,128)S(1)} %pad_maximum_fusion.refs_5_), channel_id=1, source_target_pairs={{0,4},{1,5},{2,6},{3,7},{4,0},{5,1},{6,2},{7,3},{8,12},{9,13},{10,... | collective-permute-start | bytes 589832 | tf_op jit(solution)/shard_map/ppermute | solution.py:305
  54.6 10.1 %collective-permute-start.27 = (f32[192,256]{1,0:T(8,128)S(1)}, f32[192,256]{1,0:T(8,128)S(1)}, u32[]{:S(2)}, u32[]{:S(2)}) collective-permute-start(f32[192,256]{1,0:T(8,128)S(1)} %pad_maximum_fusion.refs_5_), channel_id=1, source_target_pairs={{0,1},{1,0},{2,3},{3,2},{4,5},{5,4},{6,7},{7,6},{8,9},{9,8},{10,11... | collective-permute-start | bytes 589832 | tf_op jit(solution)/shard_map/ppermute | solution.py:305
  54.7 7.0 %collective-permute-start.23 = (f32[64,256]{1,0:T(8,128)S(1)}, f32[64,256]{1,0:T(8,128)S(1)}, u32[]{:S(2)}, u32[]{:S(2)}) collective-permute-start(f32[64,256]{1,0:T(8,128)S(1)} %fusion.2.a_ref), channel_id=1, source_target_pairs={{0,16},{1,17},{2,18},{3,19},{4,20},{5,21},{6,22},{7,23},{8,24},{9,... | collective-permute-start | bytes 196616 | tf_op jit(solution)/shard_map/ppermute | solution.py:305
  57.5 9.8 %collective-permute-start.31 = (f32[192,256]{1,0:T(8,128)S(1)}, f32[192,256]{1,0:T(8,128)S(1)}, u32[]{:S(2)}, u32[]{:S(2)}) collective-permute-start(f32[192,256]{1,0:T(8,128)S(1)} %collective-permute-done.16.refs_9_), channel_id=1, source_target_pairs={{0,1},{1,0},{2,3},{3,2},{4,5},{5,4},{6,7},{7,6},{8,9},{9,8},{10,11... | collective-permute-start | bytes 589832 | tf_op jit(solution)/shard_map/ppermute | solution.py:305
  61.6 5.8 %collective-permute-start.32 = (f32[192,256]{1,0:T(8,128)S(1)}, f32[192,256]{1,0:T(8,128)S(1)}, u32[]{:S(2)}, u32[]{:S(2)}) collective-permute-start(f32[192,256]{1,0:T(8,128)S(1)} %collective-permute-done.17.refs_10_), channel_id=1, source_target_pairs={{0,1},{1,0},{2,3},{3,2},{4,5},{5,4},{6,7},{7,6},{8,9},{9,8},{10,11... | collective-permute-start | bytes 589832 | tf_op jit(solution)/shard_map/ppermute | solution.py:305
  62.0 5.2 %collective-permute-start.24 = (f32[64,256]{1,0:T(8,128)S(1)}, f32[64,256]{1,0:T(8,128)S(1)}, u32[]{:S(2)}, u32[]{:S(2)}) collective-permute-start(f32[64,256]{1,0:T(8,128)S(1)} %right.5), channel_id=1, source_target_pairs={{0,2},{1,3},{2,0},{3,1},{4,6},{5,7},{6,4},{7,5},{8,10},{9,11},{10,... | collective-permute-start | bytes 196616 | tf_op jit(solution)/shard_map/ppermute | solution.py:305
  64.5 5.0 %collective-permute-start.28 = (f32[192,256]{1,0:T(8,128)S(1)}, f32[192,256]{1,0:T(8,128)S(1)}, u32[]{:S(2)}, u32[]{:S(2)}) collective-permute-start(f32[192,256]{1,0:T(8,128)S(1)} %collective-permute-done.7.refs_6_), channel_id=1, source_target_pairs={{0,1},{1,0},{2,3},{3,2},{4,5},{5,4},{6,7},{7,6},{8,9},{9,8},{10,11... | collective-permute-start | bytes 589832 | tf_op jit(solution)/shard_map/ppermute | solution.py:305
  64.7 9.2 %collective-permute-start.38 = (f32[192,256]{1,0:T(8,128)S(1)}, f32[192,256]{1,0:T(8,128)S(1)}, u32[]{:S(2)}, u32[]{:S(2)}) collective-permute-start(f32[192,256]{1,0:T(8,128)S(1)} %collective-permute-done.16.refs_9_), channel_id=1, source_target_pairs={{0,2},{1,3},{2,0},{3,1},{4,6},{5,7},{6,4},{7,5},{8,10},{9,11},{10,... | collective-permute-start | bytes 589832 | tf_op jit(solution)/shard_map/ppermute | solution.py:305
  67.2 2.3 %collective-permute-start.29 = (f32[192,256]{1,0:T(8,128)S(1)}, f32[192,256]{1,0:T(8,128)S(1)}, u32[]{:S(2)}, u32[]{:S(2)}) collective-permute-start(f32[192,256]{1,0:T(8,128)S(1)} %collective-permute-done.8.refs_7_), channel_id=1, source_target_pairs={{0,1},{1,0},{2,3},{3,2},{4,5},{5,4},{6,7},{7,6},{8,9},{9,8},{10,11... | collective-permute-start | bytes 589832 | tf_op jit(solution)/shard_map/ppermute | solution.py:305
  67.3 6.4 %collective-permute-start.25 = (f32[128,256]{1,0:T(8,128)S(1)}, f32[128,256]{1,0:T(8,128)S(1)}, u32[]{:S(2)}, u32[]{:S(2)}) collective-permute-start(f32[128,256]{1,0:T(8,128)S(1)} %pad_maximum_fusion.2.refs_11_), channel_id=1, source_target_pairs={{0,4},{1,5},{2,6},{3,7},{4,0},{5,1},{6,2},{7,3},{8,12},{9,13},{10,... | collective-permute-start | bytes 393224 | tf_op jit(solution)/shard_map/ppermute | solution.py:305
  67.5 6.4 %collective-permute-start.26 = (f32[128,256]{1,0:T(8,128)S(1)}, f32[128,256]{1,0:T(8,128)S(1)}, u32[]{:S(2)}, u32[]{:S(2)}) collective-permute-start(f32[128,256]{1,0:T(8,128)S(1)} %pad_maximum_fusion.2.refs_11_), channel_id=1, source_target_pairs={{0,8},{1,9},{2,10},{3,11},{4,12},{5,13},{6,14},{7,15},{8,0},{9,1},... | collective-permute-start | bytes 393224 | tf_op jit(solution)/shard_map/ppermute | solution.py:305
  69.5 8.0 %collective-permute-start.36 = (f32[192,256]{1,0:T(8,128)S(1)}, f32[192,256]{1,0:T(8,128)S(1)}, u32[]{:S(2)}, u32[]{:S(2)}) collective-permute-start(f32[192,256]{1,0:T(8,128)S(1)} %collective-permute-done.7.refs_6_), channel_id=1, source_target_pairs={{0,4},{1,5},{2,6},{3,7},{4,0},{5,1},{6,2},{7,3},{8,12},{9,13},{10,... | collective-permute-start | bytes 589832 | tf_op jit(solution)/shard_map/ppermute | solution.py:305
  69.5 7.9 %collective-permute-start.33 = (f32[128,256]{1,0:T(8,128)S(1)}, f32[128,256]{1,0:T(8,128)S(1)}, u32[]{:S(2)}, u32[]{:S(2)}) collective-permute-start(f32[128,256]{1,0:T(8,128)S(1)} %pad_maximum_fusion.2.refs_11_), channel_id=1, source_target_pairs={{0,1},{1,0},{2,3},{3,2},{4,5},{5,4},{6,7},{7,6},{8,9},{9,8},{10,11... | collective-permute-start | bytes 393224 | tf_op jit(solution)/shard_map/ppermute | solution.py:305
  73.7 5.0 %collective-permute-start.40 = (f32[128,256]{1,0:T(8,128)S(1)}, f32[128,256]{1,0:T(8,128)S(1)}, u32[]{:S(2)}, u32[]{:S(2)}) collective-permute-start(f32[128,256]{1,0:T(8,128)S(1)} %collective-permute-done.25.refs_12_), channel_id=1, source_target_pairs={{0,8},{1,9},{2,10},{3,11},{4,12},{5,13},{6,14},{7,15},{8,0},{9,1},... | collective-permute-start | bytes 393224 | tf_op jit(solution)/shard_map/ppermute | solution.py:305
  73.9 4.8 %collective-permute-start.34 = (f32[128,256]{1,0:T(8,128)S(1)}, f32[128,256]{1,0:T(8,128)S(1)}, u32[]{:S(2)}, u32[]{:S(2)}) collective-permute-start(f32[128,256]{1,0:T(8,128)S(1)} %collective-permute-done.25.refs_12_), channel_id=1, source_target_pairs={{0,1},{1,0},{2,3},{3,2},{4,5},{5,4},{6,7},{7,6},{8,9},{9,8},{10,11... | collective-permute-start | bytes 393224 | tf_op jit(solution)/shard_map/ppermute | solution.py:305
  73.9 4.8 %collective-permute-start.35 = (f32[128,256]{1,0:T(8,128)S(1)}, f32[128,256]{1,0:T(8,128)S(1)}, u32[]{:S(2)}, u32[]{:S(2)}) collective-permute-start(f32[128,256]{1,0:T(8,128)S(1)} %collective-permute-done.26.refs_13_), channel_id=1, source_target_pairs={{0,1},{1,0},{2,3},{3,2},{4,5},{5,4},{6,7},{7,6},{8,9},{9,8},{10,11... | collective-permute-start | bytes 393224 | tf_op jit(solution)/shard_map/ppermute | solution.py:305
  77.4 7.1 %collective-permute-start.39 = (f32[192,256]{1,0:T(8,128)S(1)}, f32[192,256]{1,0:T(8,128)S(1)}, u32[]{:S(2)}, u32[]{:S(2)}) collective-permute-start(f32[192,256]{1,0:T(8,128)S(1)} %collective-permute-done.38.refs_6_), channel_id=1, source_target_pairs={{0,1},{1,0},{2,3},{3,2},{4,5},{5,4},{6,7},{7,6},{8,9},{9,8},{10,11... | collective-permute-start | bytes 589832 | tf_op jit(solution)/shard_map/ppermute | solution.py:305
  77.4 7.1 %collective-permute-start.37 = (f32[192,256]{1,0:T(8,128)S(1)}, f32[192,256]{1,0:T(8,128)S(1)}, u32[]{:S(2)}, u32[]{:S(2)}) collective-permute-start(f32[192,256]{1,0:T(8,128)S(1)} %collective-permute-done.36.refs_5_), channel_id=1, source_target_pairs={{0,1},{1,0},{2,3},{3,2},{4,5},{5,4},{6,7},{7,6},{8,9},{9,8},{10,11... | collective-permute-start | bytes 589832 | tf_op jit(solution)/shard_map/ppermute | solution.py:305
  78.7 5.9 %collective-permute-start.41 = (f32[128,256]{1,0:T(8,128)S(1)}, f32[128,256]{1,0:T(8,128)S(1)}, u32[]{:S(2)}, u32[]{:S(2)}) collective-permute-start(f32[128,256]{1,0:T(8,128)S(1)} %collective-permute-done.40.refs_7_), channel_id=1, source_target_pairs={{0,1},{1,0},{2,3},{3,2},{4,5},{5,4},{6,7},{7,6},{8,9},{9,8},{10,11... | collective-permute-start | bytes 393224 | tf_op jit(solution)/shard_map/ppermute | solution.py:305
